TPU v7x, 32 devices: a whole 2x2x4 slice. The times are simulated.
32 devices in a mesh: grp: 1, ev: 32 (over z, y, x, core).
Axes of the slice: x: 2, y: 2, z: 4, core: 2. Of those that a mesh axis runs over, the one named last changes fastest.
Arguments:
- windows: bfloat16 [256, 3, 64, 1024], P(('grp', 'ev')), may hold values from -400 to 400, as said below
- rotation: bfloat16 [256, 3, 64], P(('grp', 'ev')), may hold values from -3 to 3
- source_inverse: bfloat16 [256, 1024], P(('grp', 'ev')), may hold values from -3.4 to 3.4
- send_rows: int32 [1024, 64], P(('grp', 'ev')), may hold values from 0 to 511, as said below
- tile_station: int32 [2048], P(('grp', 'ev')), may hold values from 0 to 63, as said below
- tile_count: int32 [2048], P(('grp', 'ev')), may hold values from 16 to 128
- pair_rows: int32 [2, 262144], P(None, ('grp', 'ev')), may hold values from 0 to 2047, as said below
Outputs:
- correlation: float32 [262144, 255], P(('grp', 'ev'))
Inputs may be any that keep to these rules, and one draw needn't show every extreme that they name: Each event's windows carry a scale of their own, and each station's another. `send_rows`: row j of the block of device o names the rows of device o sent to device j, each as local event times 64 plus station, with the station of the tile whose residue matches the receiving slot (o * 64 + k) mod 64. `tile_station`: tile t of a device is fed by received slots r with r mod 64 = t mod 64, all at the tile's station. `pair_rows`: entries count the rows a device receives by sending device then slot; both members of a slot lie at its tile's station.
All inputs are finite; a program needn't handle non-finite values.
Results may differ from a plain program's by a relative error of at most 0.007.
Values may be sent and summed in bfloat16 or wider, within the bound.
No kernel may reach another device: no remote copies, remote signals or barrier semaphores. Data moves between devices by JAX's collectives and lax.ppermute only.
A program may use at most 64 MiB of HBM per device.

v0:
```python
from functools import partial
import math

import jax
import jax.numpy as jnp
import numpy as np
from jax import lax
from jax.experimental import pallas as pl
from jax.experimental.pallas import tpu as pltpu
from jax.sharding import PartitionSpec as P


LAGS = 255
SUB = 8
LANES = 128
SPLIT = (5, 3)
TOGETHER = 8
SMALL = 20 << 20


epsilon = 1e-06
F32 = jnp.float32
BF16 = jnp.bfloat16


def spectral_table(length):
    half_len = length // 2
    samples = np.arange(length)[:, None]
    frequency = np.arange(half_len)[None, :]
    angles = (samples * frequency % length) * (2.0 * math.pi / length)
    factor = 1.0 / math.sqrt(length)
    table = np.concatenate([np.cos(angles) * factor, -np.sin(angles) * factor], axis=1)
    return jnp.asarray(table.astype(np.float32)).astype(BF16)


def lag_table(length, lag_count, width):
    half_len = length // 2
    frequency = np.arange(half_len)[:, None]
    shifts = np.arange(lag_count)[None, :] - lag_count // 2
    angles = (frequency * shifts % length) * (2.0 * math.pi / length)
    factor = 1.0 / math.sqrt(half_len)
    table = np.concatenate([np.cos(angles) * factor, -np.sin(angles) * factor], axis=0)
    table = np.pad(table, ((0, 0), (0, width - lag_count)))
    return jnp.asarray(table.astype(np.float32)).astype(BF16)


def column(values):
    return jnp.transpose(jnp.broadcast_to(values, (LANES, LANES)))


def one_hot(values, width):
    down = column(values)
    lane = lax.broadcasted_iota(jnp.int32, (LANES, LANES), 1)
    parts = [
        jnp.where(down == lane + LANES * j, 1.0, 0.0).astype(BF16) for j in range(width // LANES)
    ]
    return jnp.concatenate(parts, axis=1)


def spectra_kernel(steps, half_ref, win_ref, rot_ref, inv_ref, table_ref, index_ref, rows_ref, power_ref):
    step = pl.program_id(0)
    events, comps, stations, length = win_ref.shape
    half_len = length // 2
    blocks = []
    turns = rot_ref[...].astype(F32)
    for e in range(events):
        turn = turns[:, e, :]
        for s in range(1, steps):
            turn = jnp.where(step == s, turns[:, s * events + e, :], turn)
        rot = jnp.transpose(turn)
        total = rot[:, 0:1] * win_ref[e, 0].astype(F32)
        for c in range(1, comps):
            total += rot[:, c : c + 1] * win_ref[e, c].astype(F32)
        blocks.append(total.astype(BF16))
    transverse = jnp.concatenate(blocks, axis=0)
    spectrum = jnp.dot(transverse, table_ref[...], preferred_element_type=F32)
    gains = inv_ref[...].astype(F32)
    power = jnp.zeros((stations, half_len), F32)
    for e in range(events):
        re_in = spectrum[e * stations : (e + 1) * stations, :half_len]
        im_in = spectrum[e * stations : (e + 1) * stations, half_len:]
        gain = gains[e : e + 1, :]
        for s in range(1, steps):
            gain = jnp.where(step == s, gains[s * events + e : s * events + e + 1, :], gain)
        re_g, im_g = gain[:, :half_len], gain[:, half_len:]
        re = re_in * re_g - im_in * im_g
        im = re_in * im_g + im_in * re_g
        power += re * re + im * im
        base = pl.multiple_of((step * events + e) * stations, stations)
        rows_ref[pl.ds(base, stations), :half_len] = re.astype(BF16)
        rows_ref[pl.ds(base, stations), half_len:] = im.astype(BF16)

    @pl.when(step == 0)
    def _():
        power_ref[...] = power
        owners, cap = index_ref.shape
        peers = owners // 2
        other = pl.multiple_of((1 - half_ref[0]) * peers, peers)
        wanted = index_ref[pl.ds(other, peers), :]
        tail = rows_ref.shape[0] - peers
        rows_ref[tail:, :] = jnp.zeros((peers, length), BF16)
        rows_ref[tail:, :cap] = (wanted // LANES).astype(F32).astype(BF16)
        rows_ref[tail:, LANES : LANES + cap] = (wanted % LANES).astype(F32).astype(BF16)

    @pl.when(step > 0)
    def _():
        power_ref[...] += power


def event_rows(half, windows, rotation, source_inverse, send_rows, table):
    ev_dev, comps, stations, length = windows.shape
    owners, cap = send_rows.shape
    steps = 2 if ev_dev % 2 == 0 else 1
    events = ev_dev // steps
    total = ev_dev * stations + owners // 2
    args = (windows, rotation.swapaxes(0, 1), source_inverse, table, send_rows)
    args = [pltpu.with_memory_space_constraint(x, pltpu.HBM) for x in args]
    whole = lambda *shape: pl.BlockSpec(shape, lambda i, *_: (0,) * len(shape))
    return pl.pallas_call(
        partial(spectra_kernel, steps),
        grid_spec=pltpu.PrefetchScalarGridSpec(
            num_scalar_prefetch=1,
            grid=(steps,),
            in_specs=[
                pl.BlockSpec((events, comps, stations, length), lambda i, *_: (i, 0, 0, 0)),
                whole(comps, ev_dev, stations),
                whole(ev_dev, length),
                whole(length, length),
                whole(owners, cap),
            ],
            out_specs=[whole(total, length), whole(stations, length // 2)],
        ),
        out_shape=[
            jax.ShapeDtypeStruct((total, length), BF16),
            jax.ShapeDtypeStruct((stations, length // 2), F32),
        ],
        compiler_params=pltpu.CompilerParams(vmem_limit_bytes=SMALL),
        name="spectra",
    )(half, *args)


def pick_rows(index, rows, store):
    peers, cap = index.shape
    lines = LANES // cap
    for first in range(0, peers, lines):
        line = jnp.concatenate([index[first + j : first + j + 1, :] for j in range(lines)], axis=1)
        picked = jnp.dot(one_hot(line, rows.shape[0]), rows, preferred_element_type=F32)
        picked = picked.astype(BF16)
        for j in range(lines):
            store(first + j, picked[j * cap : (j + 1) * cap])


def spread(index, rows, refs, skips):
    def store(peer, picked):
        start = 0
        for ref, skip in zip(refs, skips):
            count = ref.shape[1] - skip
            ref[peer, skip:, :] = picked[start : start + count]
            start += count

    pick_rows(index, rows, store)


def own_kernel(half_ref, rows_ref, index_ref, *send_refs):
    peers = send_refs[0].shape[0]
    mine = pl.multiple_of(half_ref[0] * peers, peers)
    spread(index_ref[pl.ds(mine, peers), :], rows_ref[...], send_refs, (0, 0))


def own_sends(half, rows, send_rows, sizes):
    owners, cap = send_rows.shape
    peers = owners // 2
    length = rows.shape[1]
    whole = lambda *shape: pl.BlockSpec(shape, lambda i, *_: (0,) * len(shape))
    shapes = [(peers, size * SUB, length) for size in sizes]
    return pl.pallas_call(
        own_kernel,
        grid_spec=pltpu.PrefetchScalarGridSpec(
            num_scalar_prefetch=1,
            grid=(1,),
            in_specs=[whole(rows.shape[0] - peers, length), whole(owners, cap)],
            out_specs=[whole(*shape) for shape in shapes],
        ),
        out_shape=[jax.ShapeDtypeStruct(shape, BF16) for shape in shapes],
        compiler_params=pltpu.CompilerParams(vmem_limit_bytes=SMALL),
        name="own",
    )(half, rows, send_rows)


def relay_kernel(cap, me_ref, rows_ref, rest_ref, first_ref, *refs):
    *late_refs, held_ref = refs
    peers, kept, _ = rest_ref.shape
    tail = rows_ref.shape[0] - peers
    digits = rows_ref[tail:, :].astype(F32).astype(jnp.int32)
    index = digits[:, :cap] * LANES + digits[:, LANES : LANES + cap]
    spread(index, rows_ref[:tail, :], (first_ref, held_ref), (0, kept))
    held_ref[:, :kept, :] = rest_ref[...]
    for step, ref in enumerate(late_refs):
        ref[...] = held_ref[me_ref[0] ^ step]


def relay_sends(me, rows, rest, cap):
    peers, kept, length = rest.shape
    shapes = [(peers, cap - kept, length)] + [(2 * kept, length)] * peers
    vmem = pl.BlockSpec(memory_space=pltpu.VMEM)
    return pl.pallas_call(
        partial(relay_kernel, cap),
        in_specs=[pl.BlockSpec(memory_space=pltpu.SMEM), vmem, vmem],
        out_shape=[jax.ShapeDtypeStruct(shape, BF16) for shape in shapes],
        scratch_shapes=[pltpu.VMEM((peers, 2 * kept, length), BF16)],
        compiler_params=pltpu.CompilerParams(vmem_limit_bytes=SMALL),
        name="relay",
    )(me, rows, rest)


def place_kernel(peers, early, half_ref, me_ref, pair_ref, place_ref):
    cap = pair_ref.shape[2]
    pair = pair_ref[...]
    source = lax.div(pair, cap)
    side = lax.div(source, peers) != half_ref[0]
    offset = jnp.where(side, peers * SUB, 0)
    peer = lax.rem(source, peers)
    late = lax.broadcasted_iota(jnp.int32, pair.shape, 2) >= early * SUB
    peer = jnp.where(late, peer ^ me_ref[0], peer)
    place_ref[...] = offset + peer * SUB + lax.rem(pair, SUB)


def place_rows(half, me, pairs, peers, early):
    smem = pl.BlockSpec(memory_space=pltpu.SMEM)
    return pl.pallas_call(
        partial(place_kernel, peers, early),
        in_specs=[smem, smem, pl.BlockSpec(memory_space=pltpu.VMEM)],
        out_shape=jax.ShapeDtypeStruct(pairs.shape, jnp.int32),
        compiler_params=pltpu.CompilerParams(vmem_limit_bytes=SMALL),
        name="places",
    )(half, me, pairs)


def pair_kernel(geo, first, count, station_ref, count_ref, place_ref, weight_ref, lag_ref, *refs):
    row_refs, out_ref = refs[:count], refs[-1]
    _, cap, joint = geo
    group = pl.program_id(0) + first
    length = row_refs[0].shape[-1]
    half_len = length // 2

    rows = jnp.concatenate([ref[...].reshape(-1, length) for ref in row_refs], axis=0)
    width = rows.shape[0]
    many = TOGETHER * LANES
    for j in range(joint):
        for i in range(0, SUB, TOGETHER):
            picks = [
                one_hot(place_ref[m, j, i + n : i + n + 1, :], width)
                for m in range(2)
                for n in range(TOGETHER)
            ]
            members = jnp.dot(jnp.concatenate(picks, axis=0), rows, preferred_element_type=F32)
            halves = []
            for n in range(TOGETHER):
                a = members[n * LANES : (n + 1) * LANES]
                b = members[many + n * LANES : many + (n + 1) * LANES]
                re_a, im_a = a[:, :half_len], a[:, half_len:]
                re_b, im_b = b[:, :half_len], b[:, half_len:]
                tile = j * cap + group * SUB + i + n
                scale = weight_ref[pl.ds(station_ref[tile], 1), :]
                halves.append(
                    jnp.concatenate(
                        [
                            ((re_a * re_b + im_a * im_b) * scale).astype(BF16),
                            ((im_a * re_b - re_a * im_b) * scale).astype(BF16),
                        ],
                        axis=1,
                    )
                )
            cross = jnp.concatenate(halves, axis=0)
            lagged = jnp.concatenate(
                [
                    jnp.dot(piece, lag_ref[...], preferred_element_type=F32)
                    for piece in (cross[: many // 2], cross[many // 2 :])
                ],
                axis=0,
            )
            for n in range(TOGETHER):
                tile = j * cap + group * SUB + i + n
                piece = lagged[n * LANES : (n + 1) * LANES]
                slot = lax.broadcasted_iota(jnp.int32, piece.shape, 0)
                piece = jnp.where(slot < count_ref[tile], piece, 0.0)
                out_ref[j, (i + n) * LANES : (i + n + 1) * LANES, :] = piece[:, :LAGS]


def correlate(first, steps, sources, geo, stations_of, counts, places, weight, lag_tab, previous):
    peers, cap, joint = geo
    length = sources[0][0].shape[-1]
    in_specs = [
        pl.BlockSpec((2, joint, SUB, LANES), lambda i, *_: (0, 0, i + first, 0)),
        pl.BlockSpec(weight.shape, lambda i, *_: (0, 0)),
        pl.BlockSpec(lag_tab.shape, lambda i, *_: (0, 0)),
    ]
    args = [places, weight, lag_tab]
    for array, at in sources:
        if array.ndim == 3:
            spec = pl.BlockSpec((peers, SUB, length), lambda i, *_, at=at: (0, i + at, 0))
        else:
            spec = pl.BlockSpec((SUB, length), lambda i, *_, at=at: (i + at, 0))
        in_specs.append(spec)
        args.append(array)
    aliases = {}
    if previous is not None:
        in_specs.append(pl.BlockSpec(memory_space=pl.ANY))
        args.append(previous)
        aliases = {len(args) + 1: 0}
    tiles = joint * steps * SUB
    macs = tiles * LANES * length * (2 * 2 * peers * SUB + lag_tab.shape[1])
    return pl.pallas_call(
        partial(pair_kernel, geo, first, len(sources)),
        grid_spec=pltpu.PrefetchScalarGridSpec(
            num_scalar_prefetch=2,
            grid=(steps,),
            in_specs=in_specs,
            out_specs=pl.BlockSpec((joint, SUB * LANES, LAGS), lambda i, *_: (0, i + first, 0)),
        ),
        out_shape=jax.ShapeDtypeStruct((joint, cap * LANES, LAGS), F32),
        input_output_aliases=aliases,
        compiler_params=pltpu.CompilerParams(vmem_limit_bytes=SMALL),
        cost_estimate=pl.CostEstimate(
            flops=2 * macs, bytes_accessed=tiles * LANES * LAGS * 4, transcendentals=0
        ),
        name="pairs",
    )(stations_of, counts, *args)


def pair_up(value, step, owners):
    return lax.ppermute(value, "ev", [(i, i ^ step) for i in range(owners)])


def shards(windows, rotation, source_inverse, send_rows, tile_station, tile_count, pair_rows):
    ev_dev, _, stations, length = windows.shape
    owners = lax.axis_size("ev")
    cap = send_rows.shape[1]
    tiles_dev = tile_station.shape[0]
    joint = tiles_dev // cap
    peers = owners // 2
    half = lax.axis_index("ev") // peers
    halves = [list(range(peers)), list(range(peers, owners))]
    across = [(i, (i + peers) % owners) for i in range(owners)]
    to_peers = partial(
        lax.all_to_all,
        axis_name="ev",
        split_axis=0,
        concat_axis=0,
        axis_index_groups=halves,
        tiled=True,
    )
    half_arg = half.astype(jnp.int32).reshape(1)
    me_arg = (lax.axis_index("ev") % peers).astype(jnp.int32).reshape(1)

    rows, power = event_rows(
        half_arg, windows, rotation, source_inverse, send_rows, spectral_table(length)
    )
    groups = cap // SUB
    early = groups * SPLIT[0] // sum(SPLIT)
    sizes = (early, groups - early)
    swapped = lax.ppermute(rows, "ev", across)
    send, rest = own_sends(half_arg, rows, send_rows, sizes)
    stations = power.shape[0]
    share = stations // 2
    low = lax.axis_index("ev") % 2 == 0
    parts = power[:share], power[share:]
    kept, passed = (jnp.where(low, *parts), jnp.where(low, *parts[::-1]))
    part = kept + pair_up(passed, 1, owners)
    step = 2
    while step < peers:
        part += pair_up(part, step, owners)
        step *= 2
    own = to_peers(send)
    sends = relay_sends(me_arg, swapped, rest, cap)
    sends, own, part = lax.optimization_barrier((sends, own, part))
    part += pair_up(part, peers, owners)
    twin = pair_up(part, 1, owners)
    power = jnp.concatenate([jnp.where(low, part, twin), jnp.where(low, twin, part)], axis=0)
    weight = 1.0 / (power / (ev_dev * owners) + epsilon)
    places = place_rows(half_arg, me_arg, pair_rows.reshape(2, joint, cap, LANES), peers, early)
    lag_tab = lag_table(length, LAGS, LAGS + 1)
    geo = (peers, cap, joint)
    far = to_peers(sends[0])
    last = [sends[1]]
    for step in range(1, peers):
        last.append(pair_up(sends[1 + step], step, owners))
    run = partial(correlate, geo=geo, stations_of=tile_station, counts=tile_count, places=places)
    run = partial(run, weight=weight, lag_tab=lag_tab)
    far = pltpu.with_memory_space_constraint(far, pltpu.HBM)
    result = run(0, sizes[0], [(own, 0), (far, 0)], previous=None)
    late = [(array, at) for at in (0, sizes[1]) for array in last]
    result = run(early, sizes[1], late, previous=result)
    return result.reshape(tiles_dev * LANES, LAGS)


def solution(mesh):
    in_specs = (
        P(("grp", "ev"), None, None, None),
        P(("grp", "ev"), None, None),
        P(("grp", "ev"), None),
        P(("grp", "ev"), None),
        P(("grp", "ev")),
        P(("grp", "ev")),
        P(None, ("grp", "ev")),
    )
    out_specs = P(("grp", "ev"), None)
    return jax.shard_map(shards, mesh=mesh, in_specs=in_specs, out_specs=out_specs, check_vma=False)
```

profile of v0, /device:TPU:0, one launch (start us, length us, event | category | flops | bytes accessed | tf_op | source)
XLA Modules:
  0.0 143.7 jit_solution(17925614229206344942)
XLA Ops:
  0.0 4.5 %spectra.1 = (bf16[528,1024]{1,0:T(8,128)(2,1)S(1)}, f32[64,512]{1,0:T(8,128)S(1)}) custom-call(s32[1]{0:T(128)} %bitcast.half_ref, bf16[8,3,64,1024]{3,2,1,0:T(8,128)(2,1)} %win_ref.1, bf16[3,8,64]{2,1,0:T(8,128)(2,1)} %bitcast.11, bf16[8,1024]{1,0:T(8,128)(2,1)} %inv_ref.1, bf16[1024,1024]{1,0:T(8,128)(2,1)} %constant.56.table_ref, s32[32,64]{1,0:T(8,128)} %index_ref.3), custom_call_target="tpu_custom_call" | custom-call | tf_op jit(solution)/shard_map/spectra/pallas_call | solution.py:119
  5.2 2.4 %own.1 = (bf16[16,40,1024]{2,1,0:T(8,128)(2,1)}, bf16[16,24,1024]{2,1,0:T(8,128)(2,1)S(1)}) custom-call(s32[1]{0:T(128)} %bitcast.half_ref, bf16[528,1024]{1,0:T(8,128)(2,1)S(1)} %get-tuple-element.45.rows_ref, s32[32,64]{1,0:T(8,128)S(1)} %copy-done.6), custom_call_target="tpu_custom_call" | custom-call | tf_op jit(solution)/shard_map/own/pallas_call | solution.py:176
  7.6 0.9 copy-done
  8.5 6.3 %all-to-all-start = ((bf16[16,40,1024]{2,1,0:T(8,128)(2,1)}), bf16[16,40,1024]{2,1,0:T(8,128)(2,1)S(1)}, u32[]{:S(2)}, u32[]{:S(2)}) async-start(bf16[16,40,1024]{2,1,0:T(8,128)(2,1)} %get-tuple-element.64), calls=%async_computation | async-start | bytes 2621440 | tf_op jit(solution)/shard_map/all_to_all | solution.py:374
  14.8 2.7 %collective-permute-start = (bf16[528,1024]{1,0:T(8,128)(2,1)S(1)}, bf16[528,1024]{1,0:T(8,128)(2,1)S(1)}, u32[]{:S(2)}, u32[]{:S(2)}) collective-permute-start(bf16[528,1024]{1,0:T(8,128)(2,1)S(1)} %get-tuple-element.45.rows_ref), channel_id=1, source_target_pairs={{0,16},{1,17},{2,18},{3,19},{4,20},{5,21},{6,22},{7,23},{8,24},{9,... | collective-permute-start | bytes 3244040 | tf_op jit(solution)/shard_map/ppermute | solution.py:362
  17.5 0.9 slice_select_fusion
  18.5 1.2 collective-permute-done.1
  19.7 0.9 select_add_fusion
  20.6 1.9 %collective-permute-start.2 = (f32[32,512]{1,0:T(8,128)S(1)}, f32[32,512]{1,0:T(8,128)S(1)}, u32[]{:S(2)}, u32[]{:S(2)}) collective-permute-start(f32[32,512]{1,0:T(8,128)S(1)} %select_add_fusion), channel_id=1, source_target_pairs={{0,2},{1,3},{2,0},{3,1},{4,6},{5,7},{6,4},{7,5},{8,10},{9,11},{10,... | collective-permute-start | bytes 196616 | tf_op jit(solution)/shard_map/ppermute | solution.py:332
  22.5 4.9 %collective-permute-done.2 = f32[32,512]{1,0:T(8,128)S(1)} collective-permute-done((f32[32,512]{1,0:T(8,128)S(1)}, f32[32,512]{1,0:T(8,128)S(1)}, u32[]{:S(2)}, u32[]{:S(2)}) %collective-permute-start.2) | collective-permute-done | bytes 65568 | tf_op jit(solution)/shard_map/ppermute | solution.py:332
  27.4 0.7 collective-permute-start.3
  28.2 3.6 %collective-permute-done.3 = f32[32,512]{1,0:T(8,128)S(1)} collective-permute-done((f32[32,512]{1,0:T(8,128)S(1)}, f32[32,512]{1,0:T(8,128)S(1)}, u32[]{:S(2)}, u32[]{:S(2)}) %collective-permute-start.3) | collective-permute-done | bytes 65568 | tf_op jit(solution)/shard_map/ppermute | solution.py:332
  31.8 8.4 %collective-permute-start.4 = (f32[32,512]{1,0:T(8,128)S(1)}, f32[32,512]{1,0:T(8,128)}, u32[]{:S(2)}, u32[]{:S(2)}) collective-permute-start(f32[32,512]{1,0:T(8,128)S(1)} %add.33), channel_id=1, source_target_pairs={{0,8},{1,9},{2,10},{3,11},{4,12},{5,13},{6,14},{7,15},{8,0},{9,1},... | collective-permute-start | bytes 196616 | tf_op jit(solution)/shard_map/ppermute | solution.py:332
  40.2 14.8 %collective-permute-done.4 = f32[32,512]{1,0:T(8,128)} collective-permute-done((f32[32,512]{1,0:T(8,128)S(1)}, f32[32,512]{1,0:T(8,128)}, u32[]{:S(2)}, u32[]{:S(2)}) %collective-permute-start.4) | collective-permute-done | bytes 65568 | tf_op jit(solution)/shard_map/ppermute | solution.py:332
  55.0 1.5 %add.34 = f32[32,512]{1,0:T(8,128)} add(f32[32,512]{1,0:T(8,128)S(1)} %add.33, f32[32,512]{1,0:T(8,128)} %collective-permute-done.4) | non-fusion elementwise | flops 16384 | bytes 196608 | tf_op jit(solution)/shard_map/add | solution.py:372
  56.4 8.7 %collective-permute-done.rows_ref = bf16[528,1024]{1,0:T(8,128)(2,1)S(1)} collective-permute-done((bf16[528,1024]{1,0:T(8,128)(2,1)S(1)}, bf16[528,1024]{1,0:T(8,128)(2,1)S(1)}, u32[]{:S(2)}, u32[]{:S(2)}) %collective-permute-start) | collective-permute-done | bytes 1081376 | tf_op jit(solution)/shard_map/ppermute | solution.py:362
  65.1 1.1 copy-done.1
  66.3 2.6 %relay.1 = (bf16[16,40,1024]{2,1,0:T(8,128)(2,1)}, bf16[48,1024]{1,0:T(8,128)(2,1)S(1)}, bf16[48,1024]{1,0:T(8,128)(2,1)}, bf16[48,1024]{1,0:T(8,128)(2,1)}, bf1...) custom-call(s32[1]{0:T(128)} %bitcast.1.me_ref, ...), custom_call_target="tpu_custom_call" | custom-call | tf_op jit(solution)/shard_map/relay/pallas_call | solution.py:206
  74.7 4.5 %all-to-all-start.1 = ((bf16[16,40,1024]{2,1,0:T(8,128)(2,1)}), bf16[16,40,1024]{2,1,0:T(8,128)(2,1)}, u32[]{:S(2)}, u32[]{:S(2)}) async-start(bf16[16,40,1024]{2,1,0:T(8,128)(2,1)} %get-tuple-element.84), calls=%async_computation.1 | async-start | bytes 2621440 | tf_op jit(solution)/shard_map/all_to_all | solution.py:384
  79.3 3.1 %collective-permute-start.5 = (f32[32,512]{1,0:T(8,128)S(1)}, f32[32,512]{1,0:T(8,128)S(1)}, u32[]{:S(2)}, u32[]{:S(2)}) collective-permute-start(f32[32,512]{1,0:T(8,128)S(1)} %copy-done.26), channel_id=1, source_target_pairs={{0,16},{1,17},{2,18},{3,19},{4,20},{5,21},{6,22},{7,23},{8,24},{9,... | collective-permute-start | bytes 196616 | tf_op jit(solution)/shard_map/ppermute | solution.py:332
  82.4 13.3 %collective-permute-done.5 = f32[32,512]{1,0:T(8,128)S(1)} collective-permute-done((f32[32,512]{1,0:T(8,128)S(1)}, f32[32,512]{1,0:T(8,128)S(1)}, u32[]{:S(2)}, u32[]{:S(2)}) %collective-permute-start.5) | collective-permute-done | bytes 65568 | tf_op jit(solution)/shard_map/ppermute | solution.py:332
  96.5 1.5 %collective-permute-start.8 = (bf16[48,1024]{1,0:T(8,128)(2,1)}, bf16[48,1024]{1,0:T(8,128)(2,1)S(1)}, u32[]{:S(2)}, u32[]{:S(2)}) collective-permute-start(bf16[48,1024]{1,0:T(8,128)(2,1)} %get-tuple-element.69), channel_id=1, source_target_pairs={{0,2},{1,3},{2,0},{3,1},{4,6},{5,7},{6,4},{7,5},{8,10},{9,11},{10,... | collective-permute-start | bytes 294920 | tf_op jit(solution)/shard_map/ppermute | solution.py:332
  98.0 1.8 %collective-permute-start.10 = (bf16[48,1024]{1,0:T(8,128)(2,1)S(1)}, bf16[48,1024]{1,0:T(8,128)(2,1)S(1)}, u32[]{:S(2)}, u32[]{:S(2)}) collective-permute-start(bf16[48,1024]{1,0:T(8,128)(2,1)S(1)} %copy-done.23), channel_id=1, source_target_pairs={{0,4},{1,5},{2,6},{3,7},{4,0},{5,1},{6,2},{7,3},{8,12},{9,13},{10,... | collective-permute-start | bytes 294920 | tf_op jit(solution)/shard_map/ppermute | solution.py:332
  100.0 2.7 %collective-permute-start.12 = (bf16[48,1024]{1,0:T(8,128)(2,1)S(1)}, bf16[48,1024]{1,0:T(8,128)(2,1)S(1)}, u32[]{:S(2)}, u32[]{:S(2)}) collective-permute-start(bf16[48,1024]{1,0:T(8,128)(2,1)S(1)} %copy-done.19), channel_id=1, source_target_pairs={{0,6},{1,7},{2,4},{3,5},{4,2},{5,3},{6,0},{7,1},{8,14},{9,15},{10,... | collective-permute-start | bytes 294920 | tf_op jit(solution)/shard_map/ppermute | solution.py:332
  103.0 5.3 %collective-permute-start.14 = (bf16[48,1024]{1,0:T(8,128)(2,1)S(1)}, bf16[48,1024]{1,0:T(8,128)(2,1)S(1)}, u32[]{:S(2)}, u32[]{:S(2)}) collective-permute-start(bf16[48,1024]{1,0:T(8,128)(2,1)S(1)} %copy-done.15), channel_id=1, source_target_pairs={{0,8},{1,9},{2,10},{3,11},{4,12},{5,13},{6,14},{7,15},{8,0},{9,1},... | collective-permute-start | bytes 294920 | tf_op jit(solution)/shard_map/ppermute | solution.py:332
  108.3 1.5 %collective-permute-start.15 = (bf16[48,1024]{1,0:T(8,128)(2,1)S(1)}, bf16[48,1024]{1,0:T(8,128)(2,1)S(1)}, u32[]{:S(2)}, u32[]{:S(2)}) collective-permute-start(bf16[48,1024]{1,0:T(8,128)(2,1)S(1)} %copy-done.13), channel_id=1, source_target_pairs={{0,9},{1,8},{2,11},{3,10},{4,13},{5,12},{6,15},{7,14},{8,1},{9,0},... | collective-permute-start | bytes 294920 | tf_op jit(solution)/shard_map/ppermute | solution.py:332
  109.9 5.7 %collective-permute-start.16 = (bf16[48,1024]{1,0:T(8,128)(2,1)S(1)}, bf16[48,1024]{1,0:T(8,128)(2,1)S(1)}, u32[]{:S(2)}, u32[]{:S(2)}) collective-permute-start(bf16[48,1024]{1,0:T(8,128)(2,1)S(1)} %copy-done.11), channel_id=1, source_target_pairs={{0,10},{1,11},{2,8},{3,9},{4,14},{5,15},{6,12},{7,13},{8,2},{9,3},... | collective-permute-start | bytes 294920 | tf_op jit(solution)/shard_map/ppermute | solution.py:332
  115.7 2.8 %collective-permute-start.18 = (bf16[48,1024]{1,0:T(8,128)(2,1)}, bf16[48,1024]{1,0:T(8,128)(2,1)S(1)}, u32[]{:S(2)}, u32[]{:S(2)}) collective-permute-start(bf16[48,1024]{1,0:T(8,128)(2,1)} %get-tuple-element.79), channel_id=1, source_target_pairs={{0,12},{1,13},{2,14},{3,15},{4,8},{5,9},{6,10},{7,11},{8,4},{9,5},... | collective-permute-start | bytes 294920 | tf_op jit(solution)/shard_map/ppermute | solution.py:332
  118.6 3.3 %collective-permute-start.20 = (bf16[48,1024]{1,0:T(8,128)(2,1)}, bf16[48,1024]{1,0:T(8,128)(2,1)S(1)}, u32[]{:S(2)}, u32[]{:S(2)}) collective-permute-start(bf16[48,1024]{1,0:T(8,128)(2,1)} %get-tuple-element.81), channel_id=1, source_target_pairs={{0,14},{1,15},{2,12},{3,13},{4,10},{5,11},{6,8},{7,9},{8,6},{9,7},... | collective-permute-start | bytes 294920 | tf_op jit(solution)/shard_map/ppermute | solution.py:332
  122.0 0.8 copy-done.5
  122.9 12.9 %pairs.2.refs_32_ = f32[1,8192,255]{2,1,0:T(8,128)} custom-call(s32[64]{0:T(128)S(1)} %copy-done.7, s32[64]{0:T(128)S(1)} %copy-done.8, s32[2,1,64,128]{3,2,1,0:T(8,128)S(1)} %copy-done.5, f32[64,512]{1,0:T(8,128)S(1)} %fusion.1.weight_ref, bf16[1024,256]{1,0:T(8,128)(2,1)S(1)} %copy-done.3, bf16[16,40,1024]{2,1,0:T(8,128)(2,1)S(1)} %all-to-all-done.refs_0_, ...), custom_call_target="tpu_custom_call" | custom-call | flops 8053063680 | bytes 5222400 | tf_op jit(solution)/shard_map/pairs/pallas_call | solution.py:313
  135.8 7.9 %pairs.3 = f32[1,8192,255]{2,1,0:T(8,128)} custom-call(s32[64]{0:T(128)S(1)} %copy-done.7, s32[64]{0:T(128)S(1)} %copy-done.8, s32[2,1,64,128]{3,2,1,0:T(8,128)S(1)} %copy-done.5, f32[64,512]{1,0:T(8,128)S(1)} %fusion.1.weight_ref, bf16[1024,256]{1,0:T(8,128)(2,1)S(1)} %copy-done.3, ...), custom_call_target="tpu_custom_call", output_to_operand_aliasing={{}: (37, {})} | custom-call | flops 4831838208 | bytes 3133440 | tf_op jit(solution)/shard_map/pairs/pallas_call | solution.py:313
  (87 shorter events, 8.1 us)
Async XLA Ops:
  8.5 66.1 %all-to-all-start = ((bf16[16,40,1024]{2,1,0:T(8,128)(2,1)}), bf16[16,40,1024]{2,1,0:T(8,128)(2,1)S(1)}, u32[]{:S(2)}, u32[]{:S(2)}) async-start(bf16[16,40,1024]{2,1,0:T(8,128)(2,1)} %get-tuple-element.64), calls=%async_computation | async-start | bytes 2621440 | tf_op jit(solution)/shard_map/all_to_all | solution.py:374
  14.8 50.3 %collective-permute-start = (bf16[528,1024]{1,0:T(8,128)(2,1)S(1)}, bf16[528,1024]{1,0:T(8,128)(2,1)S(1)}, u32[]{:S(2)}, u32[]{:S(2)}) collective-permute-start(bf16[528,1024]{1,0:T(8,128)(2,1)S(1)} %get-tuple-element.45.rows_ref), channel_id=1, source_target_pairs={{0,16},{1,17},{2,18},{3,19},{4,20},{5,21},{6,22},{7,23},{8,24},{9,... | collective-permute-start | bytes 3244040 | tf_op jit(solution)/shard_map/ppermute | solution.py:362
  18.4 1.3 collective-permute-start.1
  20.6 6.8 %collective-permute-start.2 = (f32[32,512]{1,0:T(8,128)S(1)}, f32[32,512]{1,0:T(8,128)S(1)}, u32[]{:S(2)}, u32[]{:S(2)}) collective-permute-start(f32[32,512]{1,0:T(8,128)S(1)} %select_add_fusion), channel_id=1, source_target_pairs={{0,2},{1,3},{2,0},{3,1},{4,6},{5,7},{6,4},{7,5},{8,10},{9,11},{10,... | collective-permute-start | bytes 196616 | tf_op jit(solution)/shard_map/ppermute | solution.py:332
  27.4 4.3 %collective-permute-start.3 = (f32[32,512]{1,0:T(8,128)S(1)}, f32[32,512]{1,0:T(8,128)S(1)}, u32[]{:S(2)}, u32[]{:S(2)}) collective-permute-start(f32[32,512]{1,0:T(8,128)S(1)} %add.32), channel_id=1, source_target_pairs={{0,4},{1,5},{2,6},{3,7},{4,0},{5,1},{6,2},{7,3},{8,12},{9,13},{10,... | collective-permute-start | bytes 196616 | tf_op jit(solution)/shard_map/ppermute | solution.py:332
  31.8 23.2 %collective-permute-start.4 = (f32[32,512]{1,0:T(8,128)S(1)}, f32[32,512]{1,0:T(8,128)}, u32[]{:S(2)}, u32[]{:S(2)}) collective-permute-start(f32[32,512]{1,0:T(8,128)S(1)} %add.33), channel_id=1, source_target_pairs={{0,8},{1,9},{2,10},{3,11},{4,12},{5,13},{6,14},{7,15},{8,0},{9,1},... | collective-permute-start | bytes 196616 | tf_op jit(solution)/shard_map/ppermute | solution.py:332
  74.6 28.1 %copy-start.17 = (bf16[48,1024]{1,0:T(8,128)(2,1)S(1)}, bf16[48,1024]{1,0:T(8,128)(2,1)}, u32[]{:S(2)}) copy-start(bf16[48,1024]{1,0:T(8,128)(2,1)} %copy-done.16) | copy-start | bytes 294916
  74.6 28.4 %copy-start.15 = (bf16[48,1024]{1,0:T(8,128)(2,1)S(1)}, bf16[48,1024]{1,0:T(8,128)(2,1)}, u32[]{:S(2)}) copy-start(bf16[48,1024]{1,0:T(8,128)(2,1)} %copy-done.14) | copy-start | bytes 294916
  74.6 33.7 %copy-start.13 = (bf16[48,1024]{1,0:T(8,128)(2,1)S(1)}, bf16[48,1024]{1,0:T(8,128)(2,1)}, u32[]{:S(2)}) copy-start(bf16[48,1024]{1,0:T(8,128)(2,1)} %copy-done.12) | copy-start | bytes 294916
  74.7 35.2 %copy-start.11 = (bf16[48,1024]{1,0:T(8,128)(2,1)S(1)}, bf16[48,1024]{1,0:T(8,128)(2,1)}, u32[]{:S(2)}) copy-start(bf16[48,1024]{1,0:T(8,128)(2,1)} %copy-done.10) | copy-start | bytes 294916
  74.7 47.3 %copy-start.3 = (bf16[1024,256]{1,0:T(8,128)(2,1)S(1)}, bf16[1024,256]{1,0:T(8,128)(2,1)}, u32[]{:S(2)}) copy-start(bf16[1024,256]{1,0:T(8,128)(2,1)} %constant.57.lag_ref) | copy-start | bytes 1572868
  74.7 47.3 %copy-start.7 = (s32[64]{0:T(128)S(1)}, s32[64]{0:T(128)}, u32[]{:S(2)}) copy-start(s32[64]{0:T(128)} %station_ref.3) | copy-start | bytes 772
  74.7 47.3 %copy-start.8 = (s32[64]{0:T(128)S(1)}, s32[64]{0:T(128)}, u32[]{:S(2)}) copy-start(s32[64]{0:T(128)} %count_ref.3) | copy-start | bytes 772
  74.7 47.3 %all-to-all-start.1 = ((bf16[16,40,1024]{2,1,0:T(8,128)(2,1)}), bf16[16,40,1024]{2,1,0:T(8,128)(2,1)}, u32[]{:S(2)}, u32[]{:S(2)}) async-start(bf16[16,40,1024]{2,1,0:T(8,128)(2,1)} %get-tuple-element.84), calls=%async_computation.1 | async-start | bytes 2621440 | tf_op jit(solution)/shard_map/all_to_all | solution.py:384
  79.3 16.5 %collective-permute-start.5 = (f32[32,512]{1,0:T(8,128)S(1)}, f32[32,512]{1,0:T(8,128)S(1)}, u32[]{:S(2)}, u32[]{:S(2)}) collective-permute-start(f32[32,512]{1,0:T(8,128)S(1)} %copy-done.26), channel_id=1, source_target_pairs={{0,16},{1,17},{2,18},{3,19},{4,20},{5,21},{6,22},{7,23},{8,24},{9,... | collective-permute-start | bytes 196616 | tf_op jit(solution)/shard_map/ppermute | solution.py:332
  95.7 4.0 %collective-permute-start.6 = (f32[32,512]{1,0:T(8,128)S(1)}, f32[32,512]{1,0:T(8,128)S(1)}, u32[]{:S(2)}, u32[]{:S(2)}) collective-permute-start(f32[32,512]{1,0:T(8,128)S(1)} %add.35), channel_id=1, source_target_pairs={{0,1},{1,0},{2,3},{3,2},{4,5},{5,4},{6,7},{7,6},{8,9},{9,8},{10,11... | collective-permute-start | bytes 196616 | tf_op jit(solution)/shard_map/ppermute | solution.py:332
  95.9 26.0 %copy-start.4 = (s32[2,1,64,128]{3,2,1,0:T(8,128)}, s32[2,1,64,128]{3,2,1,0:T(8,128)S(1)}, u32[]{:S(2)}) copy-start(s32[2,1,64,128]{3,2,1,0:T(8,128)S(1)} %places.1.place_ref) | copy-start | bytes 196612
  95.9 4.1 %collective-permute-start.7 = (bf16[48,1024]{1,0:T(8,128)(2,1)}, bf16[48,1024]{1,0:T(8,128)(2,1)S(1)}, u32[]{:S(2)}, u32[]{:S(2)}) collective-permute-start(bf16[48,1024]{1,0:T(8,128)(2,1)} %get-tuple-element.68), channel_id=1, source_target_pairs={{0,1},{1,0},{2,3},{3,2},{4,5},{5,4},{6,7},{7,6},{8,9},{9,8},{10,11... | collective-permute-start | bytes 294920 | tf_op jit(solution)/shard_map/ppermute | solution.py:332
  96.5 6.2 %collective-permute-start.8 = (bf16[48,1024]{1,0:T(8,128)(2,1)}, bf16[48,1024]{1,0:T(8,128)(2,1)S(1)}, u32[]{:S(2)}, u32[]{:S(2)}) collective-permute-start(bf16[48,1024]{1,0:T(8,128)(2,1)} %get-tuple-element.69), channel_id=1, source_target_pairs={{0,2},{1,3},{2,0},{3,1},{4,6},{5,7},{6,4},{7,5},{8,10},{9,11},{10,... | collective-permute-start | bytes 294920 | tf_op jit(solution)/shard_map/ppermute | solution.py:332
  98.0 5.1 %collective-permute-start.9 = (bf16[48,1024]{1,0:T(8,128)(2,1)S(1)}, bf16[48,1024]{1,0:T(8,128)(2,1)S(1)}, u32[]{:S(2)}, u32[]{:S(2)}) collective-permute-start(bf16[48,1024]{1,0:T(8,128)(2,1)S(1)} %copy-done.25), channel_id=1, source_target_pairs={{0,3},{1,2},{2,1},{3,0},{4,7},{5,6},{6,5},{7,4},{8,11},{9,10},{10,... | collective-permute-start | bytes 294920 | tf_op jit(solution)/shard_map/ppermute | solution.py:332
  98.0 10.4 %collective-permute-start.10 = (bf16[48,1024]{1,0:T(8,128)(2,1)S(1)}, bf16[48,1024]{1,0:T(8,128)(2,1)S(1)}, u32[]{:S(2)}, u32[]{:S(2)}) collective-permute-start(bf16[48,1024]{1,0:T(8,128)(2,1)S(1)} %copy-done.23), channel_id=1, source_target_pairs={{0,4},{1,5},{2,6},{3,7},{4,0},{5,1},{6,2},{7,3},{8,12},{9,13},{10,... | collective-permute-start | bytes 294920 | tf_op jit(solution)/shard_map/ppermute | solution.py:332
  99.7 10.2 %collective-permute-start.11 = (bf16[48,1024]{1,0:T(8,128)(2,1)S(1)}, bf16[48,1024]{1,0:T(8,128)(2,1)S(1)}, u32[]{:S(2)}, u32[]{:S(2)}) collective-permute-start(bf16[48,1024]{1,0:T(8,128)(2,1)S(1)} %copy-done.21), channel_id=1, source_target_pairs={{0,5},{1,4},{2,7},{3,6},{4,1},{5,0},{6,3},{7,2},{8,13},{9,12},{10,... | collective-permute-start | bytes 294920 | tf_op jit(solution)/shard_map/ppermute | solution.py:332
  100.0 15.6 %collective-permute-start.12 = (bf16[48,1024]{1,0:T(8,128)(2,1)S(1)}, bf16[48,1024]{1,0:T(8,128)(2,1)S(1)}, u32[]{:S(2)}, u32[]{:S(2)}) collective-permute-start(bf16[48,1024]{1,0:T(8,128)(2,1)S(1)} %copy-done.19), channel_id=1, source_target_pairs={{0,6},{1,7},{2,4},{3,5},{4,2},{5,3},{6,0},{7,1},{8,14},{9,15},{10,... | collective-permute-start | bytes 294920 | tf_op jit(solution)/shard_map/ppermute | solution.py:332
  102.7 13.0 %collective-permute-start.13 = (bf16[48,1024]{1,0:T(8,128)(2,1)S(1)}, bf16[48,1024]{1,0:T(8,128)(2,1)S(1)}, u32[]{:S(2)}, u32[]{:S(2)}) collective-permute-start(bf16[48,1024]{1,0:T(8,128)(2,1)S(1)} %copy-done.17), channel_id=1, source_target_pairs={{0,7},{1,6},{2,5},{3,4},{4,3},{5,2},{6,1},{7,0},{8,15},{9,14},{10,... | collective-permute-start | bytes 294920 | tf_op jit(solution)/shard_map/ppermute | solution.py:332
  103.0 15.5 %collective-permute-start.14 = (bf16[48,1024]{1,0:T(8,128)(2,1)S(1)}, bf16[48,1024]{1,0:T(8,128)(2,1)S(1)}, u32[]{:S(2)}, u32[]{:S(2)}) collective-permute-start(bf16[48,1024]{1,0:T(8,128)(2,1)S(1)} %copy-done.15), channel_id=1, source_target_pairs={{0,8},{1,9},{2,10},{3,11},{4,12},{5,13},{6,14},{7,15},{8,0},{9,1},... | collective-permute-start | bytes 294920 | tf_op jit(solution)/shard_map/ppermute | solution.py:332
  108.3 10.3 %collective-permute-start.15 = (bf16[48,1024]{1,0:T(8,128)(2,1)S(1)}, bf16[48,1024]{1,0:T(8,128)(2,1)S(1)}, u32[]{:S(2)}, u32[]{:S(2)}) collective-permute-start(bf16[48,1024]{1,0:T(8,128)(2,1)S(1)} %copy-done.13), channel_id=1, source_target_pairs={{0,9},{1,8},{2,11},{3,10},{4,13},{5,12},{6,15},{7,14},{8,1},{9,0},... | collective-permute-start | bytes 294920 | tf_op jit(solution)/shard_map/ppermute | solution.py:332
  109.9 12.1 %collective-permute-start.16 = (bf16[48,1024]{1,0:T(8,128)(2,1)S(1)}, bf16[48,1024]{1,0:T(8,128)(2,1)S(1)}, u32[]{:S(2)}, u32[]{:S(2)}) collective-permute-start(bf16[48,1024]{1,0:T(8,128)(2,1)S(1)} %copy-done.11), channel_id=1, source_target_pairs={{0,10},{1,11},{2,8},{3,9},{4,14},{5,15},{6,12},{7,13},{8,2},{9,3},... | collective-permute-start | bytes 294920 | tf_op jit(solution)/shard_map/ppermute | solution.py:332
  115.6 20.2 %collective-permute-start.17 = (bf16[48,1024]{1,0:T(8,128)(2,1)}, bf16[48,1024]{1,0:T(8,128)(2,1)S(1)}, u32[]{:S(2)}, u32[]{:S(2)}) collective-permute-start(bf16[48,1024]{1,0:T(8,128)(2,1)} %get-tuple-element.78), channel_id=1, source_target_pairs={{0,11},{1,10},{2,9},{3,8},{4,15},{5,14},{6,13},{7,12},{8,3},{9,2},... | collective-permute-start | bytes 294920 | tf_op jit(solution)/shard_map/ppermute | solution.py:332
  115.7 20.1 %collective-permute-start.18 = (bf16[48,1024]{1,0:T(8,128)(2,1)}, bf16[48,1024]{1,0:T(8,128)(2,1)S(1)}, u32[]{:S(2)}, u32[]{:S(2)}) collective-permute-start(bf16[48,1024]{1,0:T(8,128)(2,1)} %get-tuple-element.79), channel_id=1, source_target_pairs={{0,12},{1,13},{2,14},{3,15},{4,8},{5,9},{6,10},{7,11},{8,4},{9,5},... | collective-permute-start | bytes 294920 | tf_op jit(solution)/shard_map/ppermute | solution.py:332
  118.5 17.3 %collective-permute-start.19 = (bf16[48,1024]{1,0:T(8,128)(2,1)}, bf16[48,1024]{1,0:T(8,128)(2,1)S(1)}, u32[]{:S(2)}, u32[]{:S(2)}) collective-permute-start(bf16[48,1024]{1,0:T(8,128)(2,1)} %get-tuple-element.80), channel_id=1, source_target_pairs={{0,13},{1,12},{2,15},{3,14},{4,9},{5,8},{6,11},{7,10},{8,5},{9,4},... | collective-permute-start | bytes 294920 | tf_op jit(solution)/shard_map/ppermute | solution.py:332
  118.6 17.2 %collective-permute-start.20 = (bf16[48,1024]{1,0:T(8,128)(2,1)}, bf16[48,1024]{1,0:T(8,128)(2,1)S(1)}, u32[]{:S(2)}, u32[]{:S(2)}) collective-permute-start(bf16[48,1024]{1,0:T(8,128)(2,1)} %get-tuple-element.81), channel_id=1, source_target_pairs={{0,14},{1,15},{2,12},{3,13},{4,10},{5,11},{6,8},{7,9},{8,6},{9,7},... | collective-permute-start | bytes 294920 | tf_op jit(solution)/shard_map/ppermute | solution.py:332
  121.9 13.9 %collective-permute-start.21 = (bf16[48,1024]{1,0:T(8,128)(2,1)}, bf16[48,1024]{1,0:T(8,128)(2,1)S(1)}, u32[]{:S(2)}, u32[]{:S(2)}) collective-permute-start(bf16[48,1024]{1,0:T(8,128)(2,1)} %copy-done.9), channel_id=1, source_target_pairs={{0,15},{1,14},{2,13},{3,12},{4,11},{5,10},{6,9},{7,8},{8,7},{9,6},... | collective-permute-start | bytes 294920 | tf_op jit(solution)/shard_map/ppermute | solution.py:332
  (20 other events, 137.5 us)
where the time goes:
time: 145 us; the launch traced here: 144 us
  starting transfers between devices  53.7 us (37%)
  waiting for transfers between devices  46.7 us (32%)
  Pallas kernels  30.4 us (21%)
  local copies, waits for them, and re-layouts  9.28 us (6%)
  other arithmetic  3.3 us (2%)
    ppermute x21, starting transfers between devices, pair_up(): return lax.ppermute(value, 'ev', [(i, i ^ step) for i in range(owners)])  40.2 us
    ppermute x21, waiting for transfers between devices, pair_up(): return lax.ppermute(value, 'ev', [(i, i ^ step) for i in range(owners)])  38 us
    pallas_call x2, Pallas kernels, correlate(): pl.pallas_call(partial(pair_kernel, geo, first, len(sources)), grid_spec=...  20.8 us
    unnamed x57, local copies, waits for them, and re-layouts  9.28 us
    ppermute x1, waiting for transfers between devices, shards(): swapped = lax.ppermute(rows, 'ev', across)  8.72 us
    all_to_all x1, starting transfers between devices, shards(): own = to_peers(send)  6.32 us
    all_to_all x1, starting transfers between devices, shards(): far = to_peers(sends[0])  4.54 us
    pallas_call x1, Pallas kernels, event_rows(): pl.pallas_call(partial(spectra_kernel, steps), grid_spec=pltpu.PrefetchSc...  4.5 us
  transfers between devices with their start and end apart: 24, of which 7 were waited for; matrix products, arithmetic and copies ran while one was open for 2% of the time, Pallas kernels for 11%

commit v1 on v0

--- a/solution.py
+++ b/solution.py
@@ -13,7 +13,7 @@
 LAGS = 255
 SUB = 8
 LANES = 128
-SPLIT = (5, 3)
+SPLIT = (6, 2)
 TOGETHER = 8
 SMALL = 20 << 20
 
@@ -187,27 +187,27 @@
     )(half, rows, send_rows)
 
 
-def relay_kernel(cap, me_ref, rows_ref, rest_ref, first_ref, *refs):
-    *late_refs, held_ref = refs
+def relay_kernel(cap, me_ref, rows_ref, rest_ref, *refs):
+    *first_refs, last_ref, held_ref = refs
     peers, kept, _ = rest_ref.shape
     tail = rows_ref.shape[0] - peers
     digits = rows_ref[tail:, :].astype(F32).astype(jnp.int32)
     index = digits[:, :cap] * LANES + digits[:, LANES : LANES + cap]
-    spread(index, rows_ref[:tail, :], (first_ref, held_ref), (0, kept))
-    held_ref[:, :kept, :] = rest_ref[...]
-    for step, ref in enumerate(late_refs):
+    spread(index, rows_ref[:tail, :], (held_ref, last_ref), (0, kept))
+    last_ref[:, :kept, :] = rest_ref[...]
+    for step, ref in enumerate(first_refs):
         ref[...] = held_ref[me_ref[0] ^ step]
 
 
 def relay_sends(me, rows, rest, cap):
     peers, kept, length = rest.shape
-    shapes = [(peers, cap - kept, length)] + [(2 * kept, length)] * peers
+    shapes = [(cap - kept, length)] * peers + [(peers, 2 * kept, length)]
     vmem = pl.BlockSpec(memory_space=pltpu.VMEM)
     return pl.pallas_call(
         partial(relay_kernel, cap),
         in_specs=[pl.BlockSpec(memory_space=pltpu.SMEM), vmem, vmem],
         out_shape=[jax.ShapeDtypeStruct(shape, BF16) for shape in shapes],
-        scratch_shapes=[pltpu.VMEM((peers, 2 * kept, length), BF16)],
+        scratch_shapes=[pltpu.VMEM((peers, cap - kept, length), BF16)],
         compiler_params=pltpu.CompilerParams(vmem_limit_bytes=SMALL),
         name="relay",
     )(me, rows, rest)
@@ -221,7 +221,7 @@
     offset = jnp.where(side, peers * SUB, 0)
     peer = lax.rem(source, peers)
     late = lax.broadcasted_iota(jnp.int32, pair.shape, 2) >= early * SUB
-    peer = jnp.where(late, peer ^ me_ref[0], peer)
+    peer = jnp.where(late | (offset == 0), peer, peer ^ me_ref[0])
     place_ref[...] = offset + peer * SUB + lax.rem(pair, SUB)
 
 
@@ -373,7 +373,6 @@
         step *= 2
     own = to_peers(send)
     sends = relay_sends(me_arg, swapped, rest, cap)
-    sends, own, part = lax.optimization_barrier((sends, own, part))
     part += pair_up(part, peers, owners)
     twin = pair_up(part, 1, owners)
     power = jnp.concatenate([jnp.where(low, part, twin), jnp.where(low, twin, part)], axis=0)
@@ -381,16 +380,14 @@
     places = place_rows(half_arg, me_arg, pair_rows.reshape(2, joint, cap, LANES), peers, early)
     lag_tab = lag_table(length, LAGS, LAGS + 1)
     geo = (peers, cap, joint)
-    far = to_peers(sends[0])
-    last = [sends[1]]
+    far = [sends[0]]
     for step in range(1, peers):
-        last.append(pair_up(sends[1 + step], step, owners))
+        far.append(pair_up(sends[step], step, owners))
+    last = to_peers(sends[peers])
     run = partial(correlate, geo=geo, stations_of=tile_station, counts=tile_count, places=places)
     run = partial(run, weight=weight, lag_tab=lag_tab)
-    far = pltpu.with_memory_space_constraint(far, pltpu.HBM)
-    result = run(0, sizes[0], [(own, 0), (far, 0)], previous=None)
-    late = [(array, at) for at in (0, sizes[1]) for array in last]
-    result = run(early, sizes[1], late, previous=result)
+    result = run(0, sizes[0], [(own, 0)] + [(array, 0) for array in far], previous=None)
+    result = run(early, sizes[1], [(last, 0), (last, sizes[1])], previous=result)
     return result.reshape(tiles_dev * LANES, LAGS)
 
 

time: 145 us -> 162 us (1.12)
  waiting for transfers between devices: 46.7 us -> 84 us
  starting transfers between devices: 53.7 us -> 37.3 us
  other arithmetic: 3.3 us -> 0.95 us
    ppermute x1, waiting for transfers between devices: 8.72 us -> 47.8 us  [shards(): swapped = lax.ppermute(rows, 'ev', across)]
    ppermute x21, starting transfers between devices: 40.2 us -> 24.2 us  [pair_up(): return lax.ppermute(value, 'ev', [(i, i ^ step) for i in range(owners)])]
    ppermute x21, waiting for transfers between devices: 38 us -> 36.1 us  [pair_up(): return lax.ppermute(value, 'ev', [(i, i ^ step) for i in range(owners)])]
    unnamed x57 -> x37, local copies, waits for them, and re-layouts: 9.28 us -> 9.32 us
  transfers between devices with their start and end apart: 24 -> 24, of which waited for: 7 -> 12; matrix products, arithmetic and copies ran while one was open for 2% -> 1% of each run, Pallas kernels for 11% -> 11%
where the time goes in v1:
time: 162 us; the launch traced here: 161 us
  waiting for transfers between devices  84 us (52%)
  starting transfers between devices  37.3 us (23%)
  Pallas kernels  29.5 us (18%)
  local copies, waits for them, and re-layouts  9.32 us (6%)
    ppermute x1, waiting for transfers between devices, shards(): swapped = lax.ppermute(rows, 'ev', across)  47.8 us
    ppermute x21, waiting for transfers between devices, pair_up(): return lax.ppermute(value, 'ev', [(i, i ^ step) for i in range(owners)])  36.1 us
    ppermute x21, starting transfers between devices, pair_up(): return lax.ppermute(value, 'ev', [(i, i ^ step) for i in range(owners)])  24.2 us
    pallas_call x2, Pallas kernels, correlate(): pl.pallas_call(partial(pair_kernel, geo, first, len(sources)), grid_spec=...  20 us
    unnamed x37, local copies, waits for them, and re-layouts  9.32 us
    all_to_all x1, starting transfers between devices, shards(): own = to_peers(send)  6.32 us
    pallas_call x1, Pallas kernels, event_rows(): pl.pallas_call(partial(spectra_kernel, steps), grid_spec=pltpu.PrefetchSc...  4.58 us
    all_to_all x1, starting transfers between devices, shards(): last = to_peers(sends[peers])  4.16 us
  transfers between devices with their start and end apart: 24, of which 12 were waited for; matrix products, arithmetic and copies ran while one was open for 1% of the time, Pallas kernels for 11%

profile of v1, /device:TPU:0, one launch (start us, length us, event | category | flops | bytes accessed | tf_op | source)
XLA Modules:
  0.0 161.2 jit_solution(4126092975377698443)
XLA Ops:
  0.0 4.6 %spectra.1 = (bf16[528,1024]{1,0:T(8,128)(2,1)S(1)}, f32[64,512]{1,0:T(8,128)S(1)}) custom-call(s32[1]{0:T(128)} %bitcast.half_ref, bf16[8,3,64,1024]{3,2,1,0:T(8,128)(2,1)} %win_ref.1, bf16[3,8,64]{2,1,0:T(8,128)(2,1)} %bitcast.11, bf16[8,1024]{1,0:T(8,128)(2,1)} %inv_ref.1, bf16[1024,1024]{1,0:T(8,128)(2,1)} %constant.56.table_ref, s32[32,64]{1,0:T(8,128)} %index_ref.3), custom_call_target="tpu_custom_call" | custom-call | tf_op jit(solution)/shard_map/spectra/pallas_call | solution.py:119
  4.6 1.4 own.1
  6.0 1.1 copy-done
  7.2 6.3 %all-to-all-start.1 = ((bf16[16,48,1024]{2,1,0:T(8,128)(2,1)}), bf16[16,48,1024]{2,1,0:T(8,128)(2,1)S(1)}, u32[]{:S(2)}, u32[]{:S(2)}) async-start(bf16[16,48,1024]{2,1,0:T(8,128)(2,1)} %copy-done), calls=%async_computation.1 | async-start | bytes 3145728 | tf_op jit(solution)/shard_map/all_to_all | solution.py:374
  13.5 2.6 %collective-permute-start.6 = (bf16[528,1024]{1,0:T(8,128)(2,1)}, bf16[528,1024]{1,0:T(8,128)(2,1)}, u32[]{:S(2)}, u32[]{:S(2)}) collective-permute-start(bf16[528,1024]{1,0:T(8,128)(2,1)} %copy-done.1), channel_id=1, source_target_pairs={{0,16},{1,17},{2,18},{3,19},{4,20},{5,21},{6,22},{7,23},{8,24},{9,... | collective-permute-start | bytes 3244040 | tf_op jit(solution)/shard_map/ppermute | solution.py:362
  16.3 47.8 %collective-permute-done.6.rows_ref = bf16[528,1024]{1,0:T(8,128)(2,1)} collective-permute-done((bf16[528,1024]{1,0:T(8,128)(2,1)}, bf16[528,1024]{1,0:T(8,128)(2,1)}, u32[]{:S(2)}, u32[]{:S(2)}) %collective-permute-start.6) | collective-permute-done | bytes 1081376 | tf_op jit(solution)/shard_map/ppermute | solution.py:362
  64.1 3.5 %relay.1 = (bf16[48,1024]{1,0:T(8,128)(2,1)S(1)}, bf16[48,1024]{1,0:T(8,128)(2,1)S(1)}, bf16[48,1024]{1,0:T(8,128)(2,1)S(1)}, bf16[48,1024]{1,0:T(8,128)(2,1)S(1...) custom-call(s32[1]{0:T(128)} %bitcast.1.me_ref, ...), custom_call_target="tpu_custom_call" | custom-call | tf_op jit(solution)/shard_map/relay/pallas_call | solution.py:206
  67.6 1.0 copy-done.2
  75.0 4.2 %all-to-all-start = ((bf16[16,32,1024]{2,1,0:T(8,128)(2,1)}), bf16[16,32,1024]{2,1,0:T(8,128)(2,1)S(1)}, u32[]{:S(2)}, u32[]{:S(2)}) async-start(bf16[16,32,1024]{2,1,0:T(8,128)(2,1)} %copy-done.2), calls=%async_computation | async-start | bytes 2097152 | tf_op jit(solution)/shard_map/all_to_all | solution.py:386
  80.0 2.0 %collective-permute-start.1 = (f32[32,512]{1,0:T(8,128)S(1)}, f32[32,512]{1,0:T(8,128)S(1)}, u32[]{:S(2)}, u32[]{:S(2)}) collective-permute-start(f32[32,512]{1,0:T(8,128)S(1)} %select_add_fusion), channel_id=1, source_target_pairs={{0,2},{1,3},{2,0},{3,1},{4,6},{5,7},{6,4},{7,5},{8,10},{9,11},{10,... | collective-permute-start | bytes 196616 | tf_op jit(solution)/shard_map/ppermute | solution.py:332
  82.0 13.7 %collective-permute-done.1 = f32[32,512]{1,0:T(8,128)S(1)} collective-permute-done((f32[32,512]{1,0:T(8,128)S(1)}, f32[32,512]{1,0:T(8,128)S(1)}, u32[]{:S(2)}, u32[]{:S(2)}) %collective-permute-start.1) | collective-permute-done | bytes 65568 | tf_op jit(solution)/shard_map/ppermute | solution.py:332
  96.4 3.6 %collective-permute-done.2 = f32[32,512]{1,0:T(8,128)S(1)} collective-permute-done((f32[32,512]{1,0:T(8,128)S(1)}, f32[32,512]{1,0:T(8,128)S(1)}, u32[]{:S(2)}, u32[]{:S(2)}) %collective-permute-start.2) | collective-permute-done | bytes 65568 | tf_op jit(solution)/shard_map/ppermute | solution.py:332
  100.0 1.2 collective-permute-start.3
  101.2 3.1 %collective-permute-done.3 = f32[32,512]{1,0:T(8,128)S(1)} collective-permute-done((f32[32,512]{1,0:T(8,128)S(1)}, f32[32,512]{1,0:T(8,128)S(1)}, u32[]{:S(2)}, u32[]{:S(2)}) %collective-permute-start.3) | collective-permute-done | bytes 65568 | tf_op jit(solution)/shard_map/ppermute | solution.py:332
  104.3 3.6 %collective-permute-start.4 = (f32[32,512]{1,0:T(8,128)S(1)}, f32[32,512]{1,0:T(8,128)S(1)}, u32[]{:S(2)}, u32[]{:S(2)}) collective-permute-start(f32[32,512]{1,0:T(8,128)S(1)} %add.34), channel_id=1, source_target_pairs={{0,16},{1,17},{2,18},{3,19},{4,20},{5,21},{6,22},{7,23},{8,24},{9,... | collective-permute-start | bytes 196616 | tf_op jit(solution)/shard_map/ppermute | solution.py:332
  108.0 2.9 %collective-permute-done.4 = f32[32,512]{1,0:T(8,128)S(1)} collective-permute-done((f32[32,512]{1,0:T(8,128)S(1)}, f32[32,512]{1,0:T(8,128)S(1)}, u32[]{:S(2)}, u32[]{:S(2)}) %collective-permute-start.4) | collective-permute-done | bytes 65568 | tf_op jit(solution)/shard_map/ppermute | solution.py:332
  111.5 1.4 collective-permute-start.9
  113.8 1.2 collective-permute-start.11
  117.4 0.9 collective-permute-start.13
  118.8 1.6 collective-permute-start.15
  120.4 4.2 %collective-permute-done.11.refs_6_ = bf16[48,1024]{1,0:T(8,128)(2,1)S(1)} collective-permute-done((bf16[48,1024]{1,0:T(8,128)(2,1)}, bf16[48,1024]{1,0:T(8,128)(2,1)S(1)}, u32[]{:S(2)}, u32[]{:S(2)}) %collective-permute-start.11) | collective-permute-done | bytes 98336 | tf_op jit(solution)/shard_map/ppermute | solution.py:332
  124.6 1.1 collective-permute-start.16
  125.8 1.6 collective-permute-start.17
  127.3 1.0 collective-permute-start.18
  128.4 1.7 %collective-permute-start.19 = (bf16[48,1024]{1,0:T(8,128)(2,1)}, bf16[48,1024]{1,0:T(8,128)(2,1)S(1)}, u32[]{:S(2)}, u32[]{:S(2)}) collective-permute-start(bf16[48,1024]{1,0:T(8,128)(2,1)} %get-tuple-element.44), channel_id=1, source_target_pairs={{0,13},{1,12},{2,15},{3,14},{4,9},{5,8},{6,11},{7,10},{8,5},{9,4},... | collective-permute-start | bytes 294920 | tf_op jit(solution)/shard_map/ppermute | solution.py:332
  130.0 2.1 %collective-permute-start.20 = (bf16[48,1024]{1,0:T(8,128)(2,1)}, bf16[48,1024]{1,0:T(8,128)(2,1)S(1)}, u32[]{:S(2)}, u32[]{:S(2)}) collective-permute-start(bf16[48,1024]{1,0:T(8,128)(2,1)} %get-tuple-element.45), channel_id=1, source_target_pairs={{0,14},{1,15},{2,12},{3,13},{4,10},{5,11},{6,8},{7,9},{8,6},{9,7},... | collective-permute-start | bytes 294920 | tf_op jit(solution)/shard_map/ppermute | solution.py:332
  132.1 1.5 collective-permute-start.21
  134.2 1.5 collective-permute-done.19.refs_14_
  135.7 3.9 %collective-permute-done.20.refs_15_ = bf16[48,1024]{1,0:T(8,128)(2,1)S(1)} collective-permute-done((bf16[48,1024]{1,0:T(8,128)(2,1)}, bf16[48,1024]{1,0:T(8,128)(2,1)S(1)}, u32[]{:S(2)}, u32[]{:S(2)}) %collective-permute-start.20) | collective-permute-done | bytes 98336 | tf_op jit(solution)/shard_map/ppermute | solution.py:332
  139.6 1.7 %collective-permute-done.21.refs_16_ = bf16[48,1024]{1,0:T(8,128)(2,1)S(1)} collective-permute-done((bf16[48,1024]{1,0:T(8,128)(2,1)}, bf16[48,1024]{1,0:T(8,128)(2,1)S(1)}, u32[]{:S(2)}, u32[]{:S(2)}) %collective-permute-start.21) | collective-permute-done | bytes 98336 | tf_op jit(solution)/shard_map/ppermute | solution.py:332
  141.2 14.2 %pairs.2.refs_2_ = f32[1,8192,255]{2,1,0:T(8,128)} custom-call(s32[64]{0:T(128)S(1)} %copy-done.5, s32[64]{0:T(128)S(1)} %copy-done.6, s32[2,1,64,128]{3,2,1,0:T(8,128)S(1)} %places.1.place_ref, f32[64,512]{1,0:T(8,128)S(1)} %fusion.1.weight_ref, bf16[1024,256]{1,0:T(8,128)(2,1)S(1)} %copy-done.3, bf16[16,48,1024]{2,1,0:T(8,128)(2,1)S(1)} %all-to-all-done.1.refs_0_, ...), custom_call_target="tpu_custom_call" | custom-call | flops 9663676416 | bytes 6266880 | tf_op jit(solution)/shard_map/pairs/pallas_call | solution.py:313
  155.5 5.8 %pairs.3 = f32[1,8192,255]{2,1,0:T(8,128)} custom-call(s32[64]{0:T(128)S(1)} %copy-done.5, s32[64]{0:T(128)S(1)} %copy-done.6, s32[2,1,64,128]{3,2,1,0:T(8,128)S(1)} %places.1.place_ref, f32[64,512]{1,0:T(8,128)S(1)} %fusion.1.weight_ref, bf16[1024,256]{1,0:T(8,128)(2,1)S(1)} %copy-done.3, ...), custom_call_target="tpu_custom_call", output_to_operand_aliasing={{}: (7, {})} | custom-call | flops 3221225472 | bytes 2088960 | tf_op jit(solution)/shard_map/pairs/pallas_call | solution.py:313
  (67 shorter events, 13.1 us)
Async XLA Ops:
  0.0 4.6 %copy-start.4 = (s32[32,64]{1,0:T(8,128)S(1)}, s32[32,64]{1,0:T(8,128)}, u32[]{:S(2)}) copy-start(s32[32,64]{1,0:T(8,128)} %index_ref.3) | copy-start | bytes 24580
  4.6 1.4 copy-start.1
  6.0 1.1 copy-start
  7.2 67.8 %all-to-all-start.1 = ((bf16[16,48,1024]{2,1,0:T(8,128)(2,1)}), bf16[16,48,1024]{2,1,0:T(8,128)(2,1)S(1)}, u32[]{:S(2)}, u32[]{:S(2)}) async-start(bf16[16,48,1024]{2,1,0:T(8,128)(2,1)} %copy-done), calls=%async_computation.1 | async-start | bytes 3145728 | tf_op jit(solution)/shard_map/all_to_all | solution.py:374
  13.5 50.6 %collective-permute-start.6 = (bf16[528,1024]{1,0:T(8,128)(2,1)}, bf16[528,1024]{1,0:T(8,128)(2,1)}, u32[]{:S(2)}, u32[]{:S(2)}) collective-permute-start(bf16[528,1024]{1,0:T(8,128)(2,1)} %copy-done.1), channel_id=1, source_target_pairs={{0,16},{1,17},{2,18},{3,19},{4,20},{5,21},{6,22},{7,23},{8,24},{9,... | collective-permute-start | bytes 3244040 | tf_op jit(solution)/shard_map/ppermute | solution.py:362
  16.1 63.0 %collective-permute-start = (f32[32,512]{1,0:T(8,128)S(1)}, f32[32,512]{1,0:T(8,128)}, u32[]{:S(2)}, u32[]{:S(2)}) collective-permute-start(f32[32,512]{1,0:T(8,128)S(1)} %slice_select_fusion), channel_id=1, source_target_pairs={{0,1},{1,0},{2,3},{3,2},{4,5},{5,4},{6,7},{7,6},{8,9},{9,8},{10,11... | collective-permute-start | bytes 196616 | tf_op jit(solution)/shard_map/ppermute | solution.py:332
  67.6 1.0 copy-start.2
  74.9 66.3 %copy-start.3 = (bf16[1024,256]{1,0:T(8,128)(2,1)S(1)}, bf16[1024,256]{1,0:T(8,128)(2,1)}, u32[]{:S(2)}) copy-start(bf16[1024,256]{1,0:T(8,128)(2,1)} %constant.57.lag_ref) | copy-start | bytes 1572868
  74.9 66.3 %copy-start.5 = (s32[64]{0:T(128)S(1)}, s32[64]{0:T(128)}, u32[]{:S(2)}) copy-start(s32[64]{0:T(128)} %station_ref.3) | copy-start | bytes 772
  74.9 66.3 %copy-start.6 = (s32[64]{0:T(128)S(1)}, s32[64]{0:T(128)}, u32[]{:S(2)}) copy-start(s32[64]{0:T(128)} %count_ref.3) | copy-start | bytes 772
  74.9 49.7 %copy-start.8 = (bf16[48,1024]{1,0:T(8,128)(2,1)S(1)}, bf16[48,1024]{1,0:T(8,128)(2,1)}, u32[]{:S(2)}) copy-start(bf16[48,1024]{1,0:T(8,128)(2,1)} %copy-done.7) | copy-start | bytes 294916
  75.0 80.5 %all-to-all-start = ((bf16[16,32,1024]{2,1,0:T(8,128)(2,1)}), bf16[16,32,1024]{2,1,0:T(8,128)(2,1)S(1)}, u32[]{:S(2)}, u32[]{:S(2)}) async-start(bf16[16,32,1024]{2,1,0:T(8,128)(2,1)} %copy-done.2), calls=%async_computation | async-start | bytes 2097152 | tf_op jit(solution)/shard_map/all_to_all | solution.py:386
  80.0 15.6 %collective-permute-start.1 = (f32[32,512]{1,0:T(8,128)S(1)}, f32[32,512]{1,0:T(8,128)S(1)}, u32[]{:S(2)}, u32[]{:S(2)}) collective-permute-start(f32[32,512]{1,0:T(8,128)S(1)} %select_add_fusion), channel_id=1, source_target_pairs={{0,2},{1,3},{2,0},{3,1},{4,6},{5,7},{6,4},{7,5},{8,10},{9,11},{10,... | collective-permute-start | bytes 196616 | tf_op jit(solution)/shard_map/ppermute | solution.py:332
  95.7 4.3 %collective-permute-start.2 = (f32[32,512]{1,0:T(8,128)S(1)}, f32[32,512]{1,0:T(8,128)S(1)}, u32[]{:S(2)}, u32[]{:S(2)}) collective-permute-start(f32[32,512]{1,0:T(8,128)S(1)} %add.32), channel_id=1, source_target_pairs={{0,4},{1,5},{2,6},{3,7},{4,0},{5,1},{6,2},{7,3},{8,12},{9,13},{10,... | collective-permute-start | bytes 196616 | tf_op jit(solution)/shard_map/ppermute | solution.py:332
  100.0 4.3 %collective-permute-start.3 = (f32[32,512]{1,0:T(8,128)S(1)}, f32[32,512]{1,0:T(8,128)S(1)}, u32[]{:S(2)}, u32[]{:S(2)}) collective-permute-start(f32[32,512]{1,0:T(8,128)S(1)} %add.33), channel_id=1, source_target_pairs={{0,8},{1,9},{2,10},{3,11},{4,12},{5,13},{6,14},{7,15},{8,0},{9,1},... | collective-permute-start | bytes 196616 | tf_op jit(solution)/shard_map/ppermute | solution.py:332
  104.3 6.6 %collective-permute-start.4 = (f32[32,512]{1,0:T(8,128)S(1)}, f32[32,512]{1,0:T(8,128)S(1)}, u32[]{:S(2)}, u32[]{:S(2)}) collective-permute-start(f32[32,512]{1,0:T(8,128)S(1)} %add.34), channel_id=1, source_target_pairs={{0,16},{1,17},{2,18},{3,19},{4,20},{5,21},{6,22},{7,23},{8,24},{9,... | collective-permute-start | bytes 196616 | tf_op jit(solution)/shard_map/ppermute | solution.py:332
  110.9 2.9 %collective-permute-start.5 = (f32[32,512]{1,0:T(8,128)S(1)}, f32[32,512]{1,0:T(8,128)S(1)}, u32[]{:S(2)}, u32[]{:S(2)}) collective-permute-start(f32[32,512]{1,0:T(8,128)S(1)} %add.35), channel_id=1, source_target_pairs={{0,1},{1,0},{2,3},{3,2},{4,5},{5,4},{6,7},{7,6},{8,9},{9,8},{10,11... | collective-permute-start | bytes 196616 | tf_op jit(solution)/shard_map/ppermute | solution.py:332
  111.0 4.9 %collective-permute-start.7 = (bf16[48,1024]{1,0:T(8,128)(2,1)}, bf16[48,1024]{1,0:T(8,128)(2,1)S(1)}, u32[]{:S(2)}, u32[]{:S(2)}) collective-permute-start(bf16[48,1024]{1,0:T(8,128)(2,1)} %copy-done.17), channel_id=1, source_target_pairs={{0,1},{1,0},{2,3},{3,2},{4,5},{5,4},{6,7},{7,6},{8,9},{9,8},{10,11... | collective-permute-start | bytes 294920 | tf_op jit(solution)/shard_map/ppermute | solution.py:332
  111.5 5.9 %collective-permute-start.8 = (bf16[48,1024]{1,0:T(8,128)(2,1)}, bf16[48,1024]{1,0:T(8,128)(2,1)S(1)}, u32[]{:S(2)}, u32[]{:S(2)}) collective-permute-start(bf16[48,1024]{1,0:T(8,128)(2,1)} %copy-done.16), channel_id=1, source_target_pairs={{0,2},{1,3},{2,0},{3,1},{4,6},{5,7},{6,4},{7,5},{8,10},{9,11},{10,... | collective-permute-start | bytes 294920 | tf_op jit(solution)/shard_map/ppermute | solution.py:332
  111.5 6.8 %collective-permute-start.9 = (bf16[48,1024]{1,0:T(8,128)(2,1)}, bf16[48,1024]{1,0:T(8,128)(2,1)S(1)}, u32[]{:S(2)}, u32[]{:S(2)}) collective-permute-start(bf16[48,1024]{1,0:T(8,128)(2,1)} %copy-done.15), channel_id=1, source_target_pairs={{0,3},{1,2},{2,1},{3,0},{4,7},{5,6},{6,5},{7,4},{8,11},{9,10},{10,... | collective-permute-start | bytes 294920 | tf_op jit(solution)/shard_map/ppermute | solution.py:332
  112.9 5.9 %collective-permute-start.10 = (bf16[48,1024]{1,0:T(8,128)(2,1)}, bf16[48,1024]{1,0:T(8,128)(2,1)S(1)}, u32[]{:S(2)}, u32[]{:S(2)}) collective-permute-start(bf16[48,1024]{1,0:T(8,128)(2,1)} %copy-done.14), channel_id=1, source_target_pairs={{0,4},{1,5},{2,6},{3,7},{4,0},{5,1},{6,2},{7,3},{8,12},{9,13},{10,... | collective-permute-start | bytes 294920 | tf_op jit(solution)/shard_map/ppermute | solution.py:332
  113.8 10.8 %collective-permute-start.11 = (bf16[48,1024]{1,0:T(8,128)(2,1)}, bf16[48,1024]{1,0:T(8,128)(2,1)S(1)}, u32[]{:S(2)}, u32[]{:S(2)}) collective-permute-start(bf16[48,1024]{1,0:T(8,128)(2,1)} %copy-done.13), channel_id=1, source_target_pairs={{0,5},{1,4},{2,7},{3,6},{4,1},{5,0},{6,3},{7,2},{8,13},{9,12},{10,... | collective-permute-start | bytes 294920 | tf_op jit(solution)/shard_map/ppermute | solution.py:332
  115.9 9.8 %collective-permute-start.12 = (bf16[48,1024]{1,0:T(8,128)(2,1)}, bf16[48,1024]{1,0:T(8,128)(2,1)S(1)}, u32[]{:S(2)}, u32[]{:S(2)}) collective-permute-start(bf16[48,1024]{1,0:T(8,128)(2,1)} %copy-done.12), channel_id=1, source_target_pairs={{0,6},{1,7},{2,4},{3,5},{4,2},{5,3},{6,0},{7,1},{8,14},{9,15},{10,... | collective-permute-start | bytes 294920 | tf_op jit(solution)/shard_map/ppermute | solution.py:332
  117.4 10.0 %collective-permute-start.13 = (bf16[48,1024]{1,0:T(8,128)(2,1)}, bf16[48,1024]{1,0:T(8,128)(2,1)S(1)}, u32[]{:S(2)}, u32[]{:S(2)}) collective-permute-start(bf16[48,1024]{1,0:T(8,128)(2,1)} %copy-done.11), channel_id=1, source_target_pairs={{0,7},{1,6},{2,5},{3,4},{4,3},{5,2},{6,1},{7,0},{8,15},{9,14},{10,... | collective-permute-start | bytes 294920 | tf_op jit(solution)/shard_map/ppermute | solution.py:332
  118.3 10.0 %collective-permute-start.14 = (bf16[48,1024]{1,0:T(8,128)(2,1)}, bf16[48,1024]{1,0:T(8,128)(2,1)S(1)}, u32[]{:S(2)}, u32[]{:S(2)}) collective-permute-start(bf16[48,1024]{1,0:T(8,128)(2,1)} %copy-done.10), channel_id=1, source_target_pairs={{0,8},{1,9},{2,10},{3,11},{4,12},{5,13},{6,14},{7,15},{8,0},{9,1},... | collective-permute-start | bytes 294920 | tf_op jit(solution)/shard_map/ppermute | solution.py:332
  118.8 11.2 %collective-permute-start.15 = (bf16[48,1024]{1,0:T(8,128)(2,1)}, bf16[48,1024]{1,0:T(8,128)(2,1)S(1)}, u32[]{:S(2)}, u32[]{:S(2)}) collective-permute-start(bf16[48,1024]{1,0:T(8,128)(2,1)} %copy-done.9), channel_id=1, source_target_pairs={{0,9},{1,8},{2,11},{3,10},{4,13},{5,12},{6,15},{7,14},{8,1},{9,0},... | collective-permute-start | bytes 294920 | tf_op jit(solution)/shard_map/ppermute | solution.py:332
  124.6 7.5 %collective-permute-start.16 = (bf16[48,1024]{1,0:T(8,128)(2,1)S(1)}, bf16[48,1024]{1,0:T(8,128)(2,1)S(1)}, u32[]{:S(2)}, u32[]{:S(2)}) collective-permute-start(bf16[48,1024]{1,0:T(8,128)(2,1)S(1)} %copy-done.8), channel_id=1, source_target_pairs={{0,10},{1,11},{2,8},{3,9},{4,14},{5,15},{6,12},{7,13},{8,2},{9,3},... | collective-permute-start | bytes 294920 | tf_op jit(solution)/shard_map/ppermute | solution.py:332
  125.8 7.8 %collective-permute-start.17 = (bf16[48,1024]{1,0:T(8,128)(2,1)}, bf16[48,1024]{1,0:T(8,128)(2,1)S(1)}, u32[]{:S(2)}, u32[]{:S(2)}) collective-permute-start(bf16[48,1024]{1,0:T(8,128)(2,1)} %get-tuple-element.42), channel_id=1, source_target_pairs={{0,11},{1,10},{2,9},{3,8},{4,15},{5,14},{6,13},{7,12},{8,3},{9,2},... | collective-permute-start | bytes 294920 | tf_op jit(solution)/shard_map/ppermute | solution.py:332
  127.3 6.8 %collective-permute-start.18 = (bf16[48,1024]{1,0:T(8,128)(2,1)}, bf16[48,1024]{1,0:T(8,128)(2,1)S(1)}, u32[]{:S(2)}, u32[]{:S(2)}) collective-permute-start(bf16[48,1024]{1,0:T(8,128)(2,1)} %get-tuple-element.43), channel_id=1, source_target_pairs={{0,12},{1,13},{2,14},{3,15},{4,8},{5,9},{6,10},{7,11},{8,4},{9,5},... | collective-permute-start | bytes 294920 | tf_op jit(solution)/shard_map/ppermute | solution.py:332
  128.4 7.3 %collective-permute-start.19 = (bf16[48,1024]{1,0:T(8,128)(2,1)}, bf16[48,1024]{1,0:T(8,128)(2,1)S(1)}, u32[]{:S(2)}, u32[]{:S(2)}) collective-permute-start(bf16[48,1024]{1,0:T(8,128)(2,1)} %get-tuple-element.44), channel_id=1, source_target_pairs={{0,13},{1,12},{2,15},{3,14},{4,9},{5,8},{6,11},{7,10},{8,5},{9,4},... | collective-permute-start | bytes 294920 | tf_op jit(solution)/shard_map/ppermute | solution.py:332
  130.0 9.6 %collective-permute-start.20 = (bf16[48,1024]{1,0:T(8,128)(2,1)}, bf16[48,1024]{1,0:T(8,128)(2,1)S(1)}, u32[]{:S(2)}, u32[]{:S(2)}) collective-permute-start(bf16[48,1024]{1,0:T(8,128)(2,1)} %get-tuple-element.45), channel_id=1, source_target_pairs={{0,14},{1,15},{2,12},{3,13},{4,10},{5,11},{6,8},{7,9},{8,6},{9,7},... | collective-permute-start | bytes 294920 | tf_op jit(solution)/shard_map/ppermute | solution.py:332
  132.1 9.2 %collective-permute-start.21 = (bf16[48,1024]{1,0:T(8,128)(2,1)}, bf16[48,1024]{1,0:T(8,128)(2,1)S(1)}, u32[]{:S(2)}, u32[]{:S(2)}) collective-permute-start(bf16[48,1024]{1,0:T(8,128)(2,1)} %get-tuple-element.46), channel_id=1, source_target_pairs={{0,15},{1,14},{2,13},{3,12},{4,11},{5,10},{6,9},{7,8},{8,7},{9,6},... | collective-permute-start | bytes 294920 | tf_op jit(solution)/shard_map/ppermute | solution.py:332
  (10 other events, 6.3 us)

commit v2 on v1

--- a/solution.py
+++ b/solution.py
@@ -181,7 +181,7 @@
             in_specs=[whole(rows.shape[0] - peers, length), whole(owners, cap)],
             out_specs=[whole(*shape) for shape in shapes],
         ),
-        out_shape=[jax.ShapeDtypeStruct(shape, BF16) for shape in shapes],
+        out_shape=[pltpu.HBM(shape, BF16) for shape in shapes],
         compiler_params=pltpu.CompilerParams(vmem_limit_bytes=SMALL),
         name="own",
     )(half, rows, send_rows)
@@ -206,7 +206,8 @@
     return pl.pallas_call(
         partial(relay_kernel, cap),
         in_specs=[pl.BlockSpec(memory_space=pltpu.SMEM), vmem, vmem],
-        out_shape=[jax.ShapeDtypeStruct(shape, BF16) for shape in shapes],
+        out_shape=[jax.ShapeDtypeStruct(shape, BF16) for shape in shapes[:-1]]
+        + [pltpu.HBM(shapes[-1], BF16)],
         scratch_shapes=[pltpu.VMEM((peers, cap - kept, length), BF16)],
         compiler_params=pltpu.CompilerParams(vmem_limit_bytes=SMALL),
         name="relay",
@@ -372,6 +373,7 @@
         part += pair_up(part, step, owners)
         step *= 2
     own = to_peers(send)
+    rest = pltpu.with_memory_space_constraint(rest, pltpu.HBM)
     sends = relay_sends(me_arg, swapped, rest, cap)
     part += pair_up(part, peers, owners)
     twin = pair_up(part, 1, owners)

time: 162 us -> 164 us (1.012)
  Pallas kernels: 29.5 us -> 31.2 us
    unnamed x37 -> x39, local copies, waits for them, and re-layouts: 9.32 us -> 9.8 us
where the time goes in v2:
time: 164 us
  waiting for transfers between devices  84.1 us (51%)
  starting transfers between devices  37.3 us (23%)
  Pallas kernels  31.2 us (19%)
  local copies, waits for them, and re-layouts  9.8 us (6%)
    ppermute x1, waiting for transfers between devices, shards(): swapped = lax.ppermute(rows, 'ev', across)  47.8 us
    ppermute x21, waiting for transfers between devices, pair_up(): return lax.ppermute(value, 'ev', [(i, i ^ step) for i in range(owners)])  36.3 us
    ppermute x21, starting transfers between devices, pair_up(): return lax.ppermute(value, 'ev', [(i, i ^ step) for i in range(owners)])  24.2 us
    pallas_call x2, Pallas kernels, correlate(): pl.pallas_call(partial(pair_kernel, geo, first, len(sources)), grid_spec=...  20 us
    unnamed x39, local copies, waits for them, and re-layouts  9.8 us
    all_to_all x1, starting transfers between devices, shards(): own = to_peers(send)  6.32 us
    pallas_call x1, Pallas kernels, event_rows(): pl.pallas_call(partial(spectra_kernel, steps), grid_spec=pltpu.PrefetchSc...  4.6 us
    all_to_all x1, starting transfers between devices, shards(): last = to_peers(sends[peers])  4.17 us
  transfers between devices with their start and end apart: 24, of which 12 were waited for; matrix products, arithmetic and copies ran while one was open for 1% of the time, Pallas kernels for 11%

profile of v2, /device:TPU:0, one launch (start us, length us, event | category | flops | bytes accessed | tf_op | source)
XLA Modules:
  0.0 163.6 jit_solution(9954900301840864122)
XLA Ops:
  0.0 4.6 %spectra.1 = (bf16[528,1024]{1,0:T(8,128)(2,1)S(1)}, f32[64,512]{1,0:T(8,128)S(1)}) custom-call(s32[1]{0:T(128)} %bitcast.half_ref, bf16[8,3,64,1024]{3,2,1,0:T(8,128)(2,1)} %win_ref.1, bf16[3,8,64]{2,1,0:T(8,128)(2,1)} %bitcast.11, bf16[8,1024]{1,0:T(8,128)(2,1)} %inv_ref.1, bf16[1024,1024]{1,0:T(8,128)(2,1)} %constant.56.table_ref, s32[32,64]{1,0:T(8,128)} %index_ref.3), custom_call_target="tpu_custom_call" | custom-call | tf_op jit(solution)/shard_map/spectra/pallas_call | solution.py:119
  4.6 2.7 %own.1 = (bf16[16,48,1024]{2,1,0:T(8,128)(2,1)}, bf16[16,16,1024]{2,1,0:T(8,128)(2,1)}) custom-call(s32[1]{0:T(128)} %bitcast.half_ref, bf16[528,1024]{1,0:T(8,128)(2,1)S(1)} %get-tuple-element.27.rows_ref, s32[32,64]{1,0:T(8,128)S(1)} %copy-done.2), custom_call_target="tpu_custom_call" | custom-call | tf_op jit(solution)/shard_map/own/pallas_call | solution.py:176
  7.3 6.3 %all-to-all-start.1 = ((bf16[16,48,1024]{2,1,0:T(8,128)(2,1)}), bf16[16,48,1024]{2,1,0:T(8,128)(2,1)S(1)}, u32[]{:S(2)}, u32[]{:S(2)}) async-start(bf16[16,48,1024]{2,1,0:T(8,128)(2,1)} %get-tuple-element.30), calls=%async_computation.1 | async-start | bytes 3145728 | tf_op jit(solution)/shard_map/all_to_all | solution.py:375
  13.7 2.7 %collective-permute-start.6 = (bf16[528,1024]{1,0:T(8,128)(2,1)}, bf16[528,1024]{1,0:T(8,128)(2,1)}, u32[]{:S(2)}, u32[]{:S(2)}) collective-permute-start(bf16[528,1024]{1,0:T(8,128)(2,1)} %copy-done), channel_id=1, source_target_pairs={{0,16},{1,17},{2,18},{3,19},{4,20},{5,21},{6,22},{7,23},{8,24},{9,... | collective-permute-start | bytes 3244040 | tf_op jit(solution)/shard_map/ppermute | solution.py:363
  16.5 47.8 %collective-permute-done.6.rows_ref = bf16[528,1024]{1,0:T(8,128)(2,1)} collective-permute-done((bf16[528,1024]{1,0:T(8,128)(2,1)}, bf16[528,1024]{1,0:T(8,128)(2,1)}, u32[]{:S(2)}, u32[]{:S(2)}) %collective-permute-start.6) | collective-permute-done | bytes 1081376 | tf_op jit(solution)/shard_map/ppermute | solution.py:363
  64.3 3.9 %relay.1 = (bf16[48,1024]{1,0:T(8,128)(2,1)S(1)}, bf16[48,1024]{1,0:T(8,128)(2,1)S(1)}, bf16[48,1024]{1,0:T(8,128)(2,1)S(1)}, bf16[48,1024]{1,0:T(8,128)(2,1)S(1...) custom-call(s32[1]{0:T(128)} %bitcast.1.me_ref, ...), custom_call_target="tpu_custom_call" | custom-call | tf_op jit(solution)/shard_map/relay/pallas_call | solution.py:206
  77.1 4.2 %all-to-all-start = ((bf16[16,32,1024]{2,1,0:T(8,128)(2,1)}), bf16[16,32,1024]{2,1,0:T(8,128)(2,1)S(1)}, u32[]{:S(2)}, u32[]{:S(2)}) async-start(bf16[16,32,1024]{2,1,0:T(8,128)(2,1)} %get-tuple-element.29), calls=%async_computation | async-start | bytes 2097152 | tf_op jit(solution)/shard_map/all_to_all | solution.py:388
  81.3 0.9 select_add_fusion
  82.2 2.0 %collective-permute-start.1 = (f32[32,512]{1,0:T(8,128)S(1)}, f32[32,512]{1,0:T(8,128)S(1)}, u32[]{:S(2)}, u32[]{:S(2)}) collective-permute-start(f32[32,512]{1,0:T(8,128)S(1)} %select_add_fusion), channel_id=1, source_target_pairs={{0,2},{1,3},{2,0},{3,1},{4,6},{5,7},{6,4},{7,5},{8,10},{9,11},{10,... | collective-permute-start | bytes 196616 | tf_op jit(solution)/shard_map/ppermute | solution.py:333
  84.1 13.7 %collective-permute-done.1 = f32[32,512]{1,0:T(8,128)S(1)} collective-permute-done((f32[32,512]{1,0:T(8,128)S(1)}, f32[32,512]{1,0:T(8,128)S(1)}, u32[]{:S(2)}, u32[]{:S(2)}) %collective-permute-start.1) | collective-permute-done | bytes 65568 | tf_op jit(solution)/shard_map/ppermute | solution.py:333
  98.6 3.6 %collective-permute-done.2 = f32[32,512]{1,0:T(8,128)S(1)} collective-permute-done((f32[32,512]{1,0:T(8,128)S(1)}, f32[32,512]{1,0:T(8,128)S(1)}, u32[]{:S(2)}, u32[]{:S(2)}) %collective-permute-start.2) | collective-permute-done | bytes 65568 | tf_op jit(solution)/shard_map/ppermute | solution.py:333
  102.2 1.2 collective-permute-start.3
  103.4 3.1 %collective-permute-done.3 = f32[32,512]{1,0:T(8,128)S(1)} collective-permute-done((f32[32,512]{1,0:T(8,128)S(1)}, f32[32,512]{1,0:T(8,128)S(1)}, u32[]{:S(2)}, u32[]{:S(2)}) %collective-permute-start.3) | collective-permute-done | bytes 65568 | tf_op jit(solution)/shard_map/ppermute | solution.py:333
  106.5 3.6 %collective-permute-start.4 = (f32[32,512]{1,0:T(8,128)S(1)}, f32[32,512]{1,0:T(8,128)S(1)}, u32[]{:S(2)}, u32[]{:S(2)}) collective-permute-start(f32[32,512]{1,0:T(8,128)S(1)} %add.34), channel_id=1, source_target_pairs={{0,16},{1,17},{2,18},{3,19},{4,20},{5,21},{6,22},{7,23},{8,24},{9,... | collective-permute-start | bytes 196616 | tf_op jit(solution)/shard_map/ppermute | solution.py:333
  110.1 2.9 %collective-permute-done.4 = f32[32,512]{1,0:T(8,128)S(1)} collective-permute-done((f32[32,512]{1,0:T(8,128)S(1)}, f32[32,512]{1,0:T(8,128)S(1)}, u32[]{:S(2)}, u32[]{:S(2)}) %collective-permute-start.4) | collective-permute-done | bytes 65568 | tf_op jit(solution)/shard_map/ppermute | solution.py:333
  113.7 1.4 collective-permute-start.9
  115.1 0.9 collective-permute-start.10
  116.0 1.2 collective-permute-start.11
  119.6 0.9 collective-permute-start.13
  121.0 1.6 collective-permute-start.15
  122.6 4.2 %collective-permute-done.11.refs_6_ = bf16[48,1024]{1,0:T(8,128)(2,1)S(1)} collective-permute-done((bf16[48,1024]{1,0:T(8,128)(2,1)}, bf16[48,1024]{1,0:T(8,128)(2,1)S(1)}, u32[]{:S(2)}, u32[]{:S(2)}) %collective-permute-start.11) | collective-permute-done | bytes 98336 | tf_op jit(solution)/shard_map/ppermute | solution.py:333
  126.8 1.1 collective-permute-start.16
  127.9 1.6 collective-permute-start.17
  129.5 1.0 collective-permute-start.18
  130.5 1.7 %collective-permute-start.19 = (bf16[48,1024]{1,0:T(8,128)(2,1)}, bf16[48,1024]{1,0:T(8,128)(2,1)S(1)}, u32[]{:S(2)}, u32[]{:S(2)}) collective-permute-start(bf16[48,1024]{1,0:T(8,128)(2,1)} %copy-done.6), channel_id=1, source_target_pairs={{0,13},{1,12},{2,15},{3,14},{4,9},{5,8},{6,11},{7,10},{8,5},{9,4},... | collective-permute-start | bytes 294920 | tf_op jit(solution)/shard_map/ppermute | solution.py:333
  132.2 2.1 %collective-permute-start.20 = (bf16[48,1024]{1,0:T(8,128)(2,1)}, bf16[48,1024]{1,0:T(8,128)(2,1)S(1)}, u32[]{:S(2)}, u32[]{:S(2)}) collective-permute-start(bf16[48,1024]{1,0:T(8,128)(2,1)} %copy-done.5), channel_id=1, source_target_pairs={{0,14},{1,15},{2,12},{3,13},{4,10},{5,11},{6,8},{7,9},{8,6},{9,7},... | collective-permute-start | bytes 294920 | tf_op jit(solution)/shard_map/ppermute | solution.py:333
  134.2 1.5 collective-permute-start.21
  136.3 1.5 collective-permute-done.19.refs_14_
  137.8 4.1 %collective-permute-done.20.refs_15_ = bf16[48,1024]{1,0:T(8,128)(2,1)S(1)} collective-permute-done((bf16[48,1024]{1,0:T(8,128)(2,1)}, bf16[48,1024]{1,0:T(8,128)(2,1)S(1)}, u32[]{:S(2)}, u32[]{:S(2)}) %collective-permute-start.20) | collective-permute-done | bytes 98336 | tf_op jit(solution)/shard_map/ppermute | solution.py:333
  142.0 1.6 collective-permute-done.21.refs_16_
  143.6 14.2 %pairs.2.refs_2_ = f32[1,8192,255]{2,1,0:T(8,128)} custom-call(s32[64]{0:T(128)S(1)} %copy-done.3, s32[64]{0:T(128)S(1)} %copy-done.4, s32[2,1,64,128]{3,2,1,0:T(8,128)S(1)} %places.1.place_ref, f32[64,512]{1,0:T(8,128)S(1)} %fusion.1.weight_ref, bf16[1024,256]{1,0:T(8,128)(2,1)S(1)} %copy-done.1, bf16[16,48,1024]{2,1,0:T(8,128)(2,1)S(1)} %all-to-all-done.1.refs_0_, ...), custom_call_target="tpu_custom_call" | custom-call | flops 9663676416 | bytes 6266880 | tf_op jit(solution)/shard_map/pairs/pallas_call | solution.py:314
  157.8 5.8 %pairs.3 = f32[1,8192,255]{2,1,0:T(8,128)} custom-call(s32[64]{0:T(128)S(1)} %copy-done.3, s32[64]{0:T(128)S(1)} %copy-done.4, s32[2,1,64,128]{3,2,1,0:T(8,128)S(1)} %places.1.place_ref, f32[64,512]{1,0:T(8,128)S(1)} %fusion.1.weight_ref, bf16[1024,256]{1,0:T(8,128)(2,1)S(1)} %copy-done.1, ...), custom_call_target="tpu_custom_call", output_to_operand_aliasing={{}: (7, {})} | custom-call | flops 3221225472 | bytes 2088960 | tf_op jit(solution)/shard_map/pairs/pallas_call | solution.py:314
  (69 shorter events, 14.0 us)
Async XLA Ops:
  0.0 4.6 %copy-start.2 = (s32[32,64]{1,0:T(8,128)S(1)}, s32[32,64]{1,0:T(8,128)}, u32[]{:S(2)}) copy-start(s32[32,64]{1,0:T(8,128)} %index_ref.3) | copy-start | bytes 24580
  4.6 2.7 %copy-start = (bf16[528,1024]{1,0:T(8,128)(2,1)}, bf16[528,1024]{1,0:T(8,128)(2,1)S(1)}, u32[]{:S(2)}) copy-start(bf16[528,1024]{1,0:T(8,128)(2,1)S(1)} %get-tuple-element.27.rows_ref) | copy-start | bytes 3244036
  7.3 69.8 %all-to-all-start.1 = ((bf16[16,48,1024]{2,1,0:T(8,128)(2,1)}), bf16[16,48,1024]{2,1,0:T(8,128)(2,1)S(1)}, u32[]{:S(2)}, u32[]{:S(2)}) async-start(bf16[16,48,1024]{2,1,0:T(8,128)(2,1)} %get-tuple-element.30), calls=%async_computation.1 | async-start | bytes 3145728 | tf_op jit(solution)/shard_map/all_to_all | solution.py:375
  13.7 50.6 %collective-permute-start.6 = (bf16[528,1024]{1,0:T(8,128)(2,1)}, bf16[528,1024]{1,0:T(8,128)(2,1)}, u32[]{:S(2)}, u32[]{:S(2)}) collective-permute-start(bf16[528,1024]{1,0:T(8,128)(2,1)} %copy-done), channel_id=1, source_target_pairs={{0,16},{1,17},{2,18},{3,19},{4,20},{5,21},{6,22},{7,23},{8,24},{9,... | collective-permute-start | bytes 3244040 | tf_op jit(solution)/shard_map/ppermute | solution.py:363
  16.3 65.0 %collective-permute-start = (f32[32,512]{1,0:T(8,128)S(1)}, f32[32,512]{1,0:T(8,128)}, u32[]{:S(2)}, u32[]{:S(2)}) collective-permute-start(f32[32,512]{1,0:T(8,128)S(1)} %slice_select_fusion), channel_id=1, source_target_pairs={{0,1},{1,0},{2,3},{3,2},{4,5},{5,4},{6,7},{7,6},{8,9},{9,8},{10,11... | collective-permute-start | bytes 196616 | tf_op jit(solution)/shard_map/ppermute | solution.py:333
  72.0 0.6 copy-start.11
  73.9 0.6 copy-start.14
  76.5 0.6 copy-start.18
  77.1 66.5 %copy-start.1 = (bf16[1024,256]{1,0:T(8,128)(2,1)S(1)}, bf16[1024,256]{1,0:T(8,128)(2,1)}, u32[]{:S(2)}) copy-start(bf16[1024,256]{1,0:T(8,128)(2,1)} %constant.57.lag_ref) | copy-start | bytes 1572868
  77.1 66.5 %copy-start.3 = (s32[64]{0:T(128)S(1)}, s32[64]{0:T(128)}, u32[]{:S(2)}) copy-start(s32[64]{0:T(128)} %station_ref.3) | copy-start | bytes 772
  77.1 66.5 %copy-start.4 = (s32[64]{0:T(128)S(1)}, s32[64]{0:T(128)}, u32[]{:S(2)}) copy-start(s32[64]{0:T(128)} %count_ref.3) | copy-start | bytes 772
  77.1 80.7 %all-to-all-start = ((bf16[16,32,1024]{2,1,0:T(8,128)(2,1)}), bf16[16,32,1024]{2,1,0:T(8,128)(2,1)S(1)}, u32[]{:S(2)}, u32[]{:S(2)}) async-start(bf16[16,32,1024]{2,1,0:T(8,128)(2,1)} %get-tuple-element.29), calls=%async_computation | async-start | bytes 2097152 | tf_op jit(solution)/shard_map/all_to_all | solution.py:388
  82.2 15.6 %collective-permute-start.1 = (f32[32,512]{1,0:T(8,128)S(1)}, f32[32,512]{1,0:T(8,128)S(1)}, u32[]{:S(2)}, u32[]{:S(2)}) collective-permute-start(f32[32,512]{1,0:T(8,128)S(1)} %select_add_fusion), channel_id=1, source_target_pairs={{0,2},{1,3},{2,0},{3,1},{4,6},{5,7},{6,4},{7,5},{8,10},{9,11},{10,... | collective-permute-start | bytes 196616 | tf_op jit(solution)/shard_map/ppermute | solution.py:333
  97.8 4.3 %collective-permute-start.2 = (f32[32,512]{1,0:T(8,128)S(1)}, f32[32,512]{1,0:T(8,128)S(1)}, u32[]{:S(2)}, u32[]{:S(2)}) collective-permute-start(f32[32,512]{1,0:T(8,128)S(1)} %add.32), channel_id=1, source_target_pairs={{0,4},{1,5},{2,6},{3,7},{4,0},{5,1},{6,2},{7,3},{8,12},{9,13},{10,... | collective-permute-start | bytes 196616 | tf_op jit(solution)/shard_map/ppermute | solution.py:333
  102.2 4.3 %collective-permute-start.3 = (f32[32,512]{1,0:T(8,128)S(1)}, f32[32,512]{1,0:T(8,128)S(1)}, u32[]{:S(2)}, u32[]{:S(2)}) collective-permute-start(f32[32,512]{1,0:T(8,128)S(1)} %add.33), channel_id=1, source_target_pairs={{0,8},{1,9},{2,10},{3,11},{4,12},{5,13},{6,14},{7,15},{8,0},{9,1},... | collective-permute-start | bytes 196616 | tf_op jit(solution)/shard_map/ppermute | solution.py:333
  106.5 6.6 %collective-permute-start.4 = (f32[32,512]{1,0:T(8,128)S(1)}, f32[32,512]{1,0:T(8,128)S(1)}, u32[]{:S(2)}, u32[]{:S(2)}) collective-permute-start(f32[32,512]{1,0:T(8,128)S(1)} %add.34), channel_id=1, source_target_pairs={{0,16},{1,17},{2,18},{3,19},{4,20},{5,21},{6,22},{7,23},{8,24},{9,... | collective-permute-start | bytes 196616 | tf_op jit(solution)/shard_map/ppermute | solution.py:333
  113.1 2.9 %collective-permute-start.5 = (f32[32,512]{1,0:T(8,128)S(1)}, f32[32,512]{1,0:T(8,128)S(1)}, u32[]{:S(2)}, u32[]{:S(2)}) collective-permute-start(f32[32,512]{1,0:T(8,128)S(1)} %add.35), channel_id=1, source_target_pairs={{0,1},{1,0},{2,3},{3,2},{4,5},{5,4},{6,7},{7,6},{8,9},{9,8},{10,11... | collective-permute-start | bytes 196616 | tf_op jit(solution)/shard_map/ppermute | solution.py:333
  113.2 4.9 %collective-permute-start.7 = (bf16[48,1024]{1,0:T(8,128)(2,1)}, bf16[48,1024]{1,0:T(8,128)(2,1)S(1)}, u32[]{:S(2)}, u32[]{:S(2)}) collective-permute-start(bf16[48,1024]{1,0:T(8,128)(2,1)} %copy-done.18), channel_id=1, source_target_pairs={{0,1},{1,0},{2,3},{3,2},{4,5},{5,4},{6,7},{7,6},{8,9},{9,8},{10,11... | collective-permute-start | bytes 294920 | tf_op jit(solution)/shard_map/ppermute | solution.py:333
  113.7 5.9 %collective-permute-start.8 = (bf16[48,1024]{1,0:T(8,128)(2,1)}, bf16[48,1024]{1,0:T(8,128)(2,1)S(1)}, u32[]{:S(2)}, u32[]{:S(2)}) collective-permute-start(bf16[48,1024]{1,0:T(8,128)(2,1)} %copy-done.17), channel_id=1, source_target_pairs={{0,2},{1,3},{2,0},{3,1},{4,6},{5,7},{6,4},{7,5},{8,10},{9,11},{10,... | collective-permute-start | bytes 294920 | tf_op jit(solution)/shard_map/ppermute | solution.py:333
  113.7 6.8 %collective-permute-start.9 = (bf16[48,1024]{1,0:T(8,128)(2,1)}, bf16[48,1024]{1,0:T(8,128)(2,1)S(1)}, u32[]{:S(2)}, u32[]{:S(2)}) collective-permute-start(bf16[48,1024]{1,0:T(8,128)(2,1)} %copy-done.16), channel_id=1, source_target_pairs={{0,3},{1,2},{2,1},{3,0},{4,7},{5,6},{6,5},{7,4},{8,11},{9,10},{10,... | collective-permute-start | bytes 294920 | tf_op jit(solution)/shard_map/ppermute | solution.py:333
  115.1 5.9 %collective-permute-start.10 = (bf16[48,1024]{1,0:T(8,128)(2,1)}, bf16[48,1024]{1,0:T(8,128)(2,1)S(1)}, u32[]{:S(2)}, u32[]{:S(2)}) collective-permute-start(bf16[48,1024]{1,0:T(8,128)(2,1)} %copy-done.15), channel_id=1, source_target_pairs={{0,4},{1,5},{2,6},{3,7},{4,0},{5,1},{6,2},{7,3},{8,12},{9,13},{10,... | collective-permute-start | bytes 294920 | tf_op jit(solution)/shard_map/ppermute | solution.py:333
  116.0 10.8 %collective-permute-start.11 = (bf16[48,1024]{1,0:T(8,128)(2,1)}, bf16[48,1024]{1,0:T(8,128)(2,1)S(1)}, u32[]{:S(2)}, u32[]{:S(2)}) collective-permute-start(bf16[48,1024]{1,0:T(8,128)(2,1)} %copy-done.14), channel_id=1, source_target_pairs={{0,5},{1,4},{2,7},{3,6},{4,1},{5,0},{6,3},{7,2},{8,13},{9,12},{10,... | collective-permute-start | bytes 294920 | tf_op jit(solution)/shard_map/ppermute | solution.py:333
  118.1 9.8 %collective-permute-start.12 = (bf16[48,1024]{1,0:T(8,128)(2,1)}, bf16[48,1024]{1,0:T(8,128)(2,1)S(1)}, u32[]{:S(2)}, u32[]{:S(2)}) collective-permute-start(bf16[48,1024]{1,0:T(8,128)(2,1)} %copy-done.13), channel_id=1, source_target_pairs={{0,6},{1,7},{2,4},{3,5},{4,2},{5,3},{6,0},{7,1},{8,14},{9,15},{10,... | collective-permute-start | bytes 294920 | tf_op jit(solution)/shard_map/ppermute | solution.py:333
  119.6 10.0 %collective-permute-start.13 = (bf16[48,1024]{1,0:T(8,128)(2,1)}, bf16[48,1024]{1,0:T(8,128)(2,1)S(1)}, u32[]{:S(2)}, u32[]{:S(2)}) collective-permute-start(bf16[48,1024]{1,0:T(8,128)(2,1)} %copy-done.12), channel_id=1, source_target_pairs={{0,7},{1,6},{2,5},{3,4},{4,3},{5,2},{6,1},{7,0},{8,15},{9,14},{10,... | collective-permute-start | bytes 294920 | tf_op jit(solution)/shard_map/ppermute | solution.py:333
  120.5 10.0 %collective-permute-start.14 = (bf16[48,1024]{1,0:T(8,128)(2,1)}, bf16[48,1024]{1,0:T(8,128)(2,1)S(1)}, u32[]{:S(2)}, u32[]{:S(2)}) collective-permute-start(bf16[48,1024]{1,0:T(8,128)(2,1)} %copy-done.11), channel_id=1, source_target_pairs={{0,8},{1,9},{2,10},{3,11},{4,12},{5,13},{6,14},{7,15},{8,0},{9,1},... | collective-permute-start | bytes 294920 | tf_op jit(solution)/shard_map/ppermute | solution.py:333
  121.0 11.2 %collective-permute-start.15 = (bf16[48,1024]{1,0:T(8,128)(2,1)}, bf16[48,1024]{1,0:T(8,128)(2,1)S(1)}, u32[]{:S(2)}, u32[]{:S(2)}) collective-permute-start(bf16[48,1024]{1,0:T(8,128)(2,1)} %copy-done.10), channel_id=1, source_target_pairs={{0,9},{1,8},{2,11},{3,10},{4,13},{5,12},{6,15},{7,14},{8,1},{9,0},... | collective-permute-start | bytes 294920 | tf_op jit(solution)/shard_map/ppermute | solution.py:333
  126.8 7.5 %collective-permute-start.16 = (bf16[48,1024]{1,0:T(8,128)(2,1)}, bf16[48,1024]{1,0:T(8,128)(2,1)S(1)}, u32[]{:S(2)}, u32[]{:S(2)}) collective-permute-start(bf16[48,1024]{1,0:T(8,128)(2,1)} %copy-done.9), channel_id=1, source_target_pairs={{0,10},{1,11},{2,8},{3,9},{4,14},{5,15},{6,12},{7,13},{8,2},{9,3},... | collective-permute-start | bytes 294920 | tf_op jit(solution)/shard_map/ppermute | solution.py:333
  127.9 7.8 %collective-permute-start.17 = (bf16[48,1024]{1,0:T(8,128)(2,1)}, bf16[48,1024]{1,0:T(8,128)(2,1)S(1)}, u32[]{:S(2)}, u32[]{:S(2)}) collective-permute-start(bf16[48,1024]{1,0:T(8,128)(2,1)} %copy-done.8), channel_id=1, source_target_pairs={{0,11},{1,10},{2,9},{3,8},{4,15},{5,14},{6,13},{7,12},{8,3},{9,2},... | collective-permute-start | bytes 294920 | tf_op jit(solution)/shard_map/ppermute | solution.py:333
  129.5 6.8 %collective-permute-start.18 = (bf16[48,1024]{1,0:T(8,128)(2,1)}, bf16[48,1024]{1,0:T(8,128)(2,1)S(1)}, u32[]{:S(2)}, u32[]{:S(2)}) collective-permute-start(bf16[48,1024]{1,0:T(8,128)(2,1)} %copy-done.7), channel_id=1, source_target_pairs={{0,12},{1,13},{2,14},{3,15},{4,8},{5,9},{6,10},{7,11},{8,4},{9,5},... | collective-permute-start | bytes 294920 | tf_op jit(solution)/shard_map/ppermute | solution.py:333
  130.5 7.3 %collective-permute-start.19 = (bf16[48,1024]{1,0:T(8,128)(2,1)}, bf16[48,1024]{1,0:T(8,128)(2,1)S(1)}, u32[]{:S(2)}, u32[]{:S(2)}) collective-permute-start(bf16[48,1024]{1,0:T(8,128)(2,1)} %copy-done.6), channel_id=1, source_target_pairs={{0,13},{1,12},{2,15},{3,14},{4,9},{5,8},{6,11},{7,10},{8,5},{9,4},... | collective-permute-start | bytes 294920 | tf_op jit(solution)/shard_map/ppermute | solution.py:333
  132.2 9.8 %collective-permute-start.20 = (bf16[48,1024]{1,0:T(8,128)(2,1)}, bf16[48,1024]{1,0:T(8,128)(2,1)S(1)}, u32[]{:S(2)}, u32[]{:S(2)}) collective-permute-start(bf16[48,1024]{1,0:T(8,128)(2,1)} %copy-done.5), channel_id=1, source_target_pairs={{0,14},{1,15},{2,12},{3,13},{4,10},{5,11},{6,8},{7,9},{8,6},{9,7},... | collective-permute-start | bytes 294920 | tf_op jit(solution)/shard_map/ppermute | solution.py:333
  134.2 9.3 %collective-permute-start.21 = (bf16[48,1024]{1,0:T(8,128)(2,1)S(1)}, bf16[48,1024]{1,0:T(8,128)(2,1)S(1)}, u32[]{:S(2)}, u32[]{:S(2)}) collective-permute-start(bf16[48,1024]{1,0:T(8,128)(2,1)S(1)} %get-tuple-element.46), channel_id=1, source_target_pairs={{0,15},{1,14},{2,13},{3,12},{4,11},{5,10},{6,9},{7,8},{8,7},{9,6},... | collective-permute-start | bytes 294920 | tf_op jit(solution)/shard_map/ppermute | solution.py:333
  (11 other events, 7.0 us)

commit v3 on v2

--- a/solution.py
+++ b/solution.py
@@ -382,9 +382,9 @@
     places = place_rows(half_arg, me_arg, pair_rows.reshape(2, joint, cap, LANES), peers, early)
     lag_tab = lag_table(length, LAGS, LAGS + 1)
     geo = (peers, cap, joint)
-    far = [sends[0]]
-    for step in range(1, peers):
-        far.append(pair_up(sends[step], step, owners))
+    far = list(sends[:peers])
+    for step in reversed(range(1, peers)):
+        far[step] = pair_up(far[step], step, owners)
     last = to_peers(sends[peers])
     run = partial(correlate, geo=geo, stations_of=tile_station, counts=tile_count, places=places)
     run = partial(run, weight=weight, lag_tab=lag_tab)

time: 164 us -> 164 us (level)
  no operation moved by 1% of the time
where the time goes in v3:
time: 164 us
  waiting for transfers between devices  84.1 us (51%)
  starting transfers between devices  37.3 us (23%)
  Pallas kernels  31.2 us (19%)
  local copies, waits for them, and re-layouts  9.8 us (6%)
    ppermute x1, waiting for transfers between devices, shards(): swapped = lax.ppermute(rows, 'ev', across)  47.8 us
    ppermute x21, waiting for transfers between devices, pair_up(): return lax.ppermute(value, 'ev', [(i, i ^ step) for i in range(owners)])  36.3 us
    ppermute x21, starting transfers between devices, pair_up(): return lax.ppermute(value, 'ev', [(i, i ^ step) for i in range(owners)])  24.2 us
    pallas_call x2, Pallas kernels, correlate(): pl.pallas_call(partial(pair_kernel, geo, first, len(sources)), grid_spec=...  20 us
    unnamed x39, local copies, waits for them, and re-layouts  9.8 us
    all_to_all x1, starting transfers between devices, shards(): own = to_peers(send)  6.32 us
    pallas_call x1, Pallas kernels, event_rows(): pl.pallas_call(partial(spectra_kernel, steps), grid_spec=pltpu.PrefetchSc...  4.6 us
    all_to_all x1, starting transfers between devices, shards(): last = to_peers(sends[peers])  4.17 us
  transfers between devices with their start and end apart: 24, of which 12 were waited for; matrix products, arithmetic and copies ran while one was open for 1% of the time, Pallas kernels for 11%

profile of v3, /device:TPU:0, one launch (start us, length us, event | category | flops | bytes accessed | tf_op | source)
XLA Modules:
  0.0 163.6 jit_solution(9954900301840864122)
XLA Ops:
  0.0 4.6 %spectra.1 = (bf16[528,1024]{1,0:T(8,128)(2,1)S(1)}, f32[64,512]{1,0:T(8,128)S(1)}) custom-call(s32[1]{0:T(128)} %bitcast.half_ref, bf16[8,3,64,1024]{3,2,1,0:T(8,128)(2,1)} %win_ref.1, bf16[3,8,64]{2,1,0:T(8,128)(2,1)} %bitcast.11, bf16[8,1024]{1,0:T(8,128)(2,1)} %inv_ref.1, bf16[1024,1024]{1,0:T(8,128)(2,1)} %constant.56.table_ref, s32[32,64]{1,0:T(8,128)} %index_ref.3), custom_call_target="tpu_custom_call" | custom-call | tf_op jit(solution)/shard_map/spectra/pallas_call | solution.py:119
  4.6 2.7 %own.1 = (bf16[16,48,1024]{2,1,0:T(8,128)(2,1)}, bf16[16,16,1024]{2,1,0:T(8,128)(2,1)}) custom-call(s32[1]{0:T(128)} %bitcast.half_ref, bf16[528,1024]{1,0:T(8,128)(2,1)S(1)} %get-tuple-element.27.rows_ref, s32[32,64]{1,0:T(8,128)S(1)} %copy-done.2), custom_call_target="tpu_custom_call" | custom-call | tf_op jit(solution)/shard_map/own/pallas_call | solution.py:176
  7.3 6.3 %all-to-all-start.1 = ((bf16[16,48,1024]{2,1,0:T(8,128)(2,1)}), bf16[16,48,1024]{2,1,0:T(8,128)(2,1)S(1)}, u32[]{:S(2)}, u32[]{:S(2)}) async-start(bf16[16,48,1024]{2,1,0:T(8,128)(2,1)} %get-tuple-element.30), calls=%async_computation.1 | async-start | bytes 3145728 | tf_op jit(solution)/shard_map/all_to_all | solution.py:375
  13.7 2.7 %collective-permute-start.6 = (bf16[528,1024]{1,0:T(8,128)(2,1)}, bf16[528,1024]{1,0:T(8,128)(2,1)}, u32[]{:S(2)}, u32[]{:S(2)}) collective-permute-start(bf16[528,1024]{1,0:T(8,128)(2,1)} %copy-done), channel_id=1, source_target_pairs={{0,16},{1,17},{2,18},{3,19},{4,20},{5,21},{6,22},{7,23},{8,24},{9,... | collective-permute-start | bytes 3244040 | tf_op jit(solution)/shard_map/ppermute | solution.py:363
  16.5 47.8 %collective-permute-done.6.rows_ref = bf16[528,1024]{1,0:T(8,128)(2,1)} collective-permute-done((bf16[528,1024]{1,0:T(8,128)(2,1)}, bf16[528,1024]{1,0:T(8,128)(2,1)}, u32[]{:S(2)}, u32[]{:S(2)}) %collective-permute-start.6) | collective-permute-done | bytes 1081376 | tf_op jit(solution)/shard_map/ppermute | solution.py:363
  64.3 3.9 %relay.1 = (bf16[48,1024]{1,0:T(8,128)(2,1)S(1)}, bf16[48,1024]{1,0:T(8,128)(2,1)S(1)}, bf16[48,1024]{1,0:T(8,128)(2,1)S(1)}, bf16[48,1024]{1,0:T(8,128)(2,1)S(1...) custom-call(s32[1]{0:T(128)} %bitcast.1.me_ref, ...), custom_call_target="tpu_custom_call" | custom-call | tf_op jit(solution)/shard_map/relay/pallas_call | solution.py:206
  77.1 4.2 %all-to-all-start = ((bf16[16,32,1024]{2,1,0:T(8,128)(2,1)}), bf16[16,32,1024]{2,1,0:T(8,128)(2,1)S(1)}, u32[]{:S(2)}, u32[]{:S(2)}) async-start(bf16[16,32,1024]{2,1,0:T(8,128)(2,1)} %get-tuple-element.29), calls=%async_computation | async-start | bytes 2097152 | tf_op jit(solution)/shard_map/all_to_all | solution.py:388
  81.3 0.9 select_add_fusion
  82.2 2.0 %collective-permute-start.1 = (f32[32,512]{1,0:T(8,128)S(1)}, f32[32,512]{1,0:T(8,128)S(1)}, u32[]{:S(2)}, u32[]{:S(2)}) collective-permute-start(f32[32,512]{1,0:T(8,128)S(1)} %select_add_fusion), channel_id=1, source_target_pairs={{0,2},{1,3},{2,0},{3,1},{4,6},{5,7},{6,4},{7,5},{8,10},{9,11},{10,... | collective-permute-start | bytes 196616 | tf_op jit(solution)/shard_map/ppermute | solution.py:333
  84.1 13.7 %collective-permute-done.1 = f32[32,512]{1,0:T(8,128)S(1)} collective-permute-done((f32[32,512]{1,0:T(8,128)S(1)}, f32[32,512]{1,0:T(8,128)S(1)}, u32[]{:S(2)}, u32[]{:S(2)}) %collective-permute-start.1) | collective-permute-done | bytes 65568 | tf_op jit(solution)/shard_map/ppermute | solution.py:333
  98.6 3.6 %collective-permute-done.2 = f32[32,512]{1,0:T(8,128)S(1)} collective-permute-done((f32[32,512]{1,0:T(8,128)S(1)}, f32[32,512]{1,0:T(8,128)S(1)}, u32[]{:S(2)}, u32[]{:S(2)}) %collective-permute-start.2) | collective-permute-done | bytes 65568 | tf_op jit(solution)/shard_map/ppermute | solution.py:333
  102.2 1.2 collective-permute-start.3
  103.4 3.1 %collective-permute-done.3 = f32[32,512]{1,0:T(8,128)S(1)} collective-permute-done((f32[32,512]{1,0:T(8,128)S(1)}, f32[32,512]{1,0:T(8,128)S(1)}, u32[]{:S(2)}, u32[]{:S(2)}) %collective-permute-start.3) | collective-permute-done | bytes 65568 | tf_op jit(solution)/shard_map/ppermute | solution.py:333
  106.5 3.6 %collective-permute-start.4 = (f32[32,512]{1,0:T(8,128)S(1)}, f32[32,512]{1,0:T(8,128)S(1)}, u32[]{:S(2)}, u32[]{:S(2)}) collective-permute-start(f32[32,512]{1,0:T(8,128)S(1)} %add.34), channel_id=1, source_target_pairs={{0,16},{1,17},{2,18},{3,19},{4,20},{5,21},{6,22},{7,23},{8,24},{9,... | collective-permute-start | bytes 196616 | tf_op jit(solution)/shard_map/ppermute | solution.py:333
  110.1 2.9 %collective-permute-done.4 = f32[32,512]{1,0:T(8,128)S(1)} collective-permute-done((f32[32,512]{1,0:T(8,128)S(1)}, f32[32,512]{1,0:T(8,128)S(1)}, u32[]{:S(2)}, u32[]{:S(2)}) %collective-permute-start.4) | collective-permute-done | bytes 65568 | tf_op jit(solution)/shard_map/ppermute | solution.py:333
  113.7 1.4 collective-permute-start.9
  115.1 0.9 collective-permute-start.10
  116.0 1.2 collective-permute-start.11
  119.6 0.9 collective-permute-start.13
  121.0 1.6 collective-permute-start.15
  122.6 4.2 %collective-permute-done.11.refs_6_ = bf16[48,1024]{1,0:T(8,128)(2,1)S(1)} collective-permute-done((bf16[48,1024]{1,0:T(8,128)(2,1)}, bf16[48,1024]{1,0:T(8,128)(2,1)S(1)}, u32[]{:S(2)}, u32[]{:S(2)}) %collective-permute-start.11) | collective-permute-done | bytes 98336 | tf_op jit(solution)/shard_map/ppermute | solution.py:333
  126.8 1.1 collective-permute-start.16
  127.9 1.6 collective-permute-start.17
  129.5 1.0 collective-permute-start.18
  130.5 1.7 %collective-permute-start.19 = (bf16[48,1024]{1,0:T(8,128)(2,1)}, bf16[48,1024]{1,0:T(8,128)(2,1)S(1)}, u32[]{:S(2)}, u32[]{:S(2)}) collective-permute-start(bf16[48,1024]{1,0:T(8,128)(2,1)} %copy-done.6), channel_id=1, source_target_pairs={{0,13},{1,12},{2,15},{3,14},{4,9},{5,8},{6,11},{7,10},{8,5},{9,4},... | collective-permute-start | bytes 294920 | tf_op jit(solution)/shard_map/ppermute | solution.py:333
  132.2 2.1 %collective-permute-start.20 = (bf16[48,1024]{1,0:T(8,128)(2,1)}, bf16[48,1024]{1,0:T(8,128)(2,1)S(1)}, u32[]{:S(2)}, u32[]{:S(2)}) collective-permute-start(bf16[48,1024]{1,0:T(8,128)(2,1)} %copy-done.5), channel_id=1, source_target_pairs={{0,14},{1,15},{2,12},{3,13},{4,10},{5,11},{6,8},{7,9},{8,6},{9,7},... | collective-permute-start | bytes 294920 | tf_op jit(solution)/shard_map/ppermute | solution.py:333
  134.2 1.5 collective-permute-start.21
  136.3 1.5 collective-permute-done.19.refs_14_
  137.8 4.1 %collective-permute-done.20.refs_15_ = bf16[48,1024]{1,0:T(8,128)(2,1)S(1)} collective-permute-done((bf16[48,1024]{1,0:T(8,128)(2,1)}, bf16[48,1024]{1,0:T(8,128)(2,1)S(1)}, u32[]{:S(2)}, u32[]{:S(2)}) %collective-permute-start.20) | collective-permute-done | bytes 98336 | tf_op jit(solution)/shard_map/ppermute | solution.py:333
  142.0 1.6 collective-permute-done.21.refs_16_
  143.6 14.2 %pairs.2.refs_2_ = f32[1,8192,255]{2,1,0:T(8,128)} custom-call(s32[64]{0:T(128)S(1)} %copy-done.3, s32[64]{0:T(128)S(1)} %copy-done.4, s32[2,1,64,128]{3,2,1,0:T(8,128)S(1)} %places.1.place_ref, f32[64,512]{1,0:T(8,128)S(1)} %fusion.1.weight_ref, bf16[1024,256]{1,0:T(8,128)(2,1)S(1)} %copy-done.1, bf16[16,48,1024]{2,1,0:T(8,128)(2,1)S(1)} %all-to-all-done.1.refs_0_, ...), custom_call_target="tpu_custom_call" | custom-call | flops 9663676416 | bytes 6266880 | tf_op jit(solution)/shard_map/pairs/pallas_call | solution.py:314
  157.8 5.8 %pairs.3 = f32[1,8192,255]{2,1,0:T(8,128)} custom-call(s32[64]{0:T(128)S(1)} %copy-done.3, s32[64]{0:T(128)S(1)} %copy-done.4, s32[2,1,64,128]{3,2,1,0:T(8,128)S(1)} %places.1.place_ref, f32[64,512]{1,0:T(8,128)S(1)} %fusion.1.weight_ref, bf16[1024,256]{1,0:T(8,128)(2,1)S(1)} %copy-done.1, ...), custom_call_target="tpu_custom_call", output_to_operand_aliasing={{}: (7, {})} | custom-call | flops 3221225472 | bytes 2088960 | tf_op jit(solution)/shard_map/pairs/pallas_call | solution.py:314
  (69 shorter events, 14.0 us)
Async XLA Ops:
  0.0 4.6 %copy-start.2 = (s32[32,64]{1,0:T(8,128)S(1)}, s32[32,64]{1,0:T(8,128)}, u32[]{:S(2)}) copy-start(s32[32,64]{1,0:T(8,128)} %index_ref.3) | copy-start | bytes 24580
  4.6 2.7 %copy-start = (bf16[528,1024]{1,0:T(8,128)(2,1)}, bf16[528,1024]{1,0:T(8,128)(2,1)S(1)}, u32[]{:S(2)}) copy-start(bf16[528,1024]{1,0:T(8,128)(2,1)S(1)} %get-tuple-element.27.rows_ref) | copy-start | bytes 3244036
  7.3 69.8 %all-to-all-start.1 = ((bf16[16,48,1024]{2,1,0:T(8,128)(2,1)}), bf16[16,48,1024]{2,1,0:T(8,128)(2,1)S(1)}, u32[]{:S(2)}, u32[]{:S(2)}) async-start(bf16[16,48,1024]{2,1,0:T(8,128)(2,1)} %get-tuple-element.30), calls=%async_computation.1 | async-start | bytes 3145728 | tf_op jit(solution)/shard_map/all_to_all | solution.py:375
  13.7 50.6 %collective-permute-start.6 = (bf16[528,1024]{1,0:T(8,128)(2,1)}, bf16[528,1024]{1,0:T(8,128)(2,1)}, u32[]{:S(2)}, u32[]{:S(2)}) collective-permute-start(bf16[528,1024]{1,0:T(8,128)(2,1)} %copy-done), channel_id=1, source_target_pairs={{0,16},{1,17},{2,18},{3,19},{4,20},{5,21},{6,22},{7,23},{8,24},{9,... | collective-permute-start | bytes 3244040 | tf_op jit(solution)/shard_map/ppermute | solution.py:363
  16.3 65.0 %collective-permute-start = (f32[32,512]{1,0:T(8,128)S(1)}, f32[32,512]{1,0:T(8,128)}, u32[]{:S(2)}, u32[]{:S(2)}) collective-permute-start(f32[32,512]{1,0:T(8,128)S(1)} %slice_select_fusion), channel_id=1, source_target_pairs={{0,1},{1,0},{2,3},{3,2},{4,5},{5,4},{6,7},{7,6},{8,9},{9,8},{10,11... | collective-permute-start | bytes 196616 | tf_op jit(solution)/shard_map/ppermute | solution.py:333
  72.0 0.6 copy-start.11
  73.9 0.6 copy-start.14
  76.5 0.6 copy-start.18
  77.1 66.5 %copy-start.1 = (bf16[1024,256]{1,0:T(8,128)(2,1)S(1)}, bf16[1024,256]{1,0:T(8,128)(2,1)}, u32[]{:S(2)}) copy-start(bf16[1024,256]{1,0:T(8,128)(2,1)} %constant.57.lag_ref) | copy-start | bytes 1572868
  77.1 66.5 %copy-start.3 = (s32[64]{0:T(128)S(1)}, s32[64]{0:T(128)}, u32[]{:S(2)}) copy-start(s32[64]{0:T(128)} %station_ref.3) | copy-start | bytes 772
  77.1 66.5 %copy-start.4 = (s32[64]{0:T(128)S(1)}, s32[64]{0:T(128)}, u32[]{:S(2)}) copy-start(s32[64]{0:T(128)} %count_ref.3) | copy-start | bytes 772
  77.1 80.7 %all-to-all-start = ((bf16[16,32,1024]{2,1,0:T(8,128)(2,1)}), bf16[16,32,1024]{2,1,0:T(8,128)(2,1)S(1)}, u32[]{:S(2)}, u32[]{:S(2)}) async-start(bf16[16,32,1024]{2,1,0:T(8,128)(2,1)} %get-tuple-element.29), calls=%async_computation | async-start | bytes 2097152 | tf_op jit(solution)/shard_map/all_to_all | solution.py:388
  82.2 15.6 %collective-permute-start.1 = (f32[32,512]{1,0:T(8,128)S(1)}, f32[32,512]{1,0:T(8,128)S(1)}, u32[]{:S(2)}, u32[]{:S(2)}) collective-permute-start(f32[32,512]{1,0:T(8,128)S(1)} %select_add_fusion), channel_id=1, source_target_pairs={{0,2},{1,3},{2,0},{3,1},{4,6},{5,7},{6,4},{7,5},{8,10},{9,11},{10,... | collective-permute-start | bytes 196616 | tf_op jit(solution)/shard_map/ppermute | solution.py:333
  97.8 4.3 %collective-permute-start.2 = (f32[32,512]{1,0:T(8,128)S(1)}, f32[32,512]{1,0:T(8,128)S(1)}, u32[]{:S(2)}, u32[]{:S(2)}) collective-permute-start(f32[32,512]{1,0:T(8,128)S(1)} %add.32), channel_id=1, source_target_pairs={{0,4},{1,5},{2,6},{3,7},{4,0},{5,1},{6,2},{7,3},{8,12},{9,13},{10,... | collective-permute-start | bytes 196616 | tf_op jit(solution)/shard_map/ppermute | solution.py:333
  102.2 4.3 %collective-permute-start.3 = (f32[32,512]{1,0:T(8,128)S(1)}, f32[32,512]{1,0:T(8,128)S(1)}, u32[]{:S(2)}, u32[]{:S(2)}) collective-permute-start(f32[32,512]{1,0:T(8,128)S(1)} %add.33), channel_id=1, source_target_pairs={{0,8},{1,9},{2,10},{3,11},{4,12},{5,13},{6,14},{7,15},{8,0},{9,1},... | collective-permute-start | bytes 196616 | tf_op jit(solution)/shard_map/ppermute | solution.py:333
  106.5 6.6 %collective-permute-start.4 = (f32[32,512]{1,0:T(8,128)S(1)}, f32[32,512]{1,0:T(8,128)S(1)}, u32[]{:S(2)}, u32[]{:S(2)}) collective-permute-start(f32[32,512]{1,0:T(8,128)S(1)} %add.34), channel_id=1, source_target_pairs={{0,16},{1,17},{2,18},{3,19},{4,20},{5,21},{6,22},{7,23},{8,24},{9,... | collective-permute-start | bytes 196616 | tf_op jit(solution)/shard_map/ppermute | solution.py:333
  113.1 2.9 %collective-permute-start.5 = (f32[32,512]{1,0:T(8,128)S(1)}, f32[32,512]{1,0:T(8,128)S(1)}, u32[]{:S(2)}, u32[]{:S(2)}) collective-permute-start(f32[32,512]{1,0:T(8,128)S(1)} %add.35), channel_id=1, source_target_pairs={{0,1},{1,0},{2,3},{3,2},{4,5},{5,4},{6,7},{7,6},{8,9},{9,8},{10,11... | collective-permute-start | bytes 196616 | tf_op jit(solution)/shard_map/ppermute | solution.py:333
  113.2 4.9 %collective-permute-start.7 = (bf16[48,1024]{1,0:T(8,128)(2,1)}, bf16[48,1024]{1,0:T(8,128)(2,1)S(1)}, u32[]{:S(2)}, u32[]{:S(2)}) collective-permute-start(bf16[48,1024]{1,0:T(8,128)(2,1)} %copy-done.18), channel_id=1, source_target_pairs={{0,1},{1,0},{2,3},{3,2},{4,5},{5,4},{6,7},{7,6},{8,9},{9,8},{10,11... | collective-permute-start | bytes 294920 | tf_op jit(solution)/shard_map/ppermute | solution.py:333
  113.7 5.9 %collective-permute-start.8 = (bf16[48,1024]{1,0:T(8,128)(2,1)}, bf16[48,1024]{1,0:T(8,128)(2,1)S(1)}, u32[]{:S(2)}, u32[]{:S(2)}) collective-permute-start(bf16[48,1024]{1,0:T(8,128)(2,1)} %copy-done.17), channel_id=1, source_target_pairs={{0,2},{1,3},{2,0},{3,1},{4,6},{5,7},{6,4},{7,5},{8,10},{9,11},{10,... | collective-permute-start | bytes 294920 | tf_op jit(solution)/shard_map/ppermute | solution.py:333
  113.7 6.8 %collective-permute-start.9 = (bf16[48,1024]{1,0:T(8,128)(2,1)}, bf16[48,1024]{1,0:T(8,128)(2,1)S(1)}, u32[]{:S(2)}, u32[]{:S(2)}) collective-permute-start(bf16[48,1024]{1,0:T(8,128)(2,1)} %copy-done.16), channel_id=1, source_target_pairs={{0,3},{1,2},{2,1},{3,0},{4,7},{5,6},{6,5},{7,4},{8,11},{9,10},{10,... | collective-permute-start | bytes 294920 | tf_op jit(solution)/shard_map/ppermute | solution.py:333
  115.1 5.9 %collective-permute-start.10 = (bf16[48,1024]{1,0:T(8,128)(2,1)}, bf16[48,1024]{1,0:T(8,128)(2,1)S(1)}, u32[]{:S(2)}, u32[]{:S(2)}) collective-permute-start(bf16[48,1024]{1,0:T(8,128)(2,1)} %copy-done.15), channel_id=1, source_target_pairs={{0,4},{1,5},{2,6},{3,7},{4,0},{5,1},{6,2},{7,3},{8,12},{9,13},{10,... | collective-permute-start | bytes 294920 | tf_op jit(solution)/shard_map/ppermute | solution.py:333
  116.0 10.8 %collective-permute-start.11 = (bf16[48,1024]{1,0:T(8,128)(2,1)}, bf16[48,1024]{1,0:T(8,128)(2,1)S(1)}, u32[]{:S(2)}, u32[]{:S(2)}) collective-permute-start(bf16[48,1024]{1,0:T(8,128)(2,1)} %copy-done.14), channel_id=1, source_target_pairs={{0,5},{1,4},{2,7},{3,6},{4,1},{5,0},{6,3},{7,2},{8,13},{9,12},{10,... | collective-permute-start | bytes 294920 | tf_op jit(solution)/shard_map/ppermute | solution.py:333
  118.1 9.8 %collective-permute-start.12 = (bf16[48,1024]{1,0:T(8,128)(2,1)}, bf16[48,1024]{1,0:T(8,128)(2,1)S(1)}, u32[]{:S(2)}, u32[]{:S(2)}) collective-permute-start(bf16[48,1024]{1,0:T(8,128)(2,1)} %copy-done.13), channel_id=1, source_target_pairs={{0,6},{1,7},{2,4},{3,5},{4,2},{5,3},{6,0},{7,1},{8,14},{9,15},{10,... | collective-permute-start | bytes 294920 | tf_op jit(solution)/shard_map/ppermute | solution.py:333
  119.6 10.0 %collective-permute-start.13 = (bf16[48,1024]{1,0:T(8,128)(2,1)}, bf16[48,1024]{1,0:T(8,128)(2,1)S(1)}, u32[]{:S(2)}, u32[]{:S(2)}) collective-permute-start(bf16[48,1024]{1,0:T(8,128)(2,1)} %copy-done.12), channel_id=1, source_target_pairs={{0,7},{1,6},{2,5},{3,4},{4,3},{5,2},{6,1},{7,0},{8,15},{9,14},{10,... | collective-permute-start | bytes 294920 | tf_op jit(solution)/shard_map/ppermute | solution.py:333
  120.5 10.0 %collective-permute-start.14 = (bf16[48,1024]{1,0:T(8,128)(2,1)}, bf16[48,1024]{1,0:T(8,128)(2,1)S(1)}, u32[]{:S(2)}, u32[]{:S(2)}) collective-permute-start(bf16[48,1024]{1,0:T(8,128)(2,1)} %copy-done.11), channel_id=1, source_target_pairs={{0,8},{1,9},{2,10},{3,11},{4,12},{5,13},{6,14},{7,15},{8,0},{9,1},... | collective-permute-start | bytes 294920 | tf_op jit(solution)/shard_map/ppermute | solution.py:333
  121.0 11.2 %collective-permute-start.15 = (bf16[48,1024]{1,0:T(8,128)(2,1)}, bf16[48,1024]{1,0:T(8,128)(2,1)S(1)}, u32[]{:S(2)}, u32[]{:S(2)}) collective-permute-start(bf16[48,1024]{1,0:T(8,128)(2,1)} %copy-done.10), channel_id=1, source_target_pairs={{0,9},{1,8},{2,11},{3,10},{4,13},{5,12},{6,15},{7,14},{8,1},{9,0},... | collective-permute-start | bytes 294920 | tf_op jit(solution)/shard_map/ppermute | solution.py:333
  126.8 7.5 %collective-permute-start.16 = (bf16[48,1024]{1,0:T(8,128)(2,1)}, bf16[48,1024]{1,0:T(8,128)(2,1)S(1)}, u32[]{:S(2)}, u32[]{:S(2)}) collective-permute-start(bf16[48,1024]{1,0:T(8,128)(2,1)} %copy-done.9), channel_id=1, source_target_pairs={{0,10},{1,11},{2,8},{3,9},{4,14},{5,15},{6,12},{7,13},{8,2},{9,3},... | collective-permute-start | bytes 294920 | tf_op jit(solution)/shard_map/ppermute | solution.py:333
  127.9 7.8 %collective-permute-start.17 = (bf16[48,1024]{1,0:T(8,128)(2,1)}, bf16[48,1024]{1,0:T(8,128)(2,1)S(1)}, u32[]{:S(2)}, u32[]{:S(2)}) collective-permute-start(bf16[48,1024]{1,0:T(8,128)(2,1)} %copy-done.8), channel_id=1, source_target_pairs={{0,11},{1,10},{2,9},{3,8},{4,15},{5,14},{6,13},{7,12},{8,3},{9,2},... | collective-permute-start | bytes 294920 | tf_op jit(solution)/shard_map/ppermute | solution.py:333
  129.5 6.8 %collective-permute-start.18 = (bf16[48,1024]{1,0:T(8,128)(2,1)}, bf16[48,1024]{1,0:T(8,128)(2,1)S(1)}, u32[]{:S(2)}, u32[]{:S(2)}) collective-permute-start(bf16[48,1024]{1,0:T(8,128)(2,1)} %copy-done.7), channel_id=1, source_target_pairs={{0,12},{1,13},{2,14},{3,15},{4,8},{5,9},{6,10},{7,11},{8,4},{9,5},... | collective-permute-start | bytes 294920 | tf_op jit(solution)/shard_map/ppermute | solution.py:333
  130.5 7.3 %collective-permute-start.19 = (bf16[48,1024]{1,0:T(8,128)(2,1)}, bf16[48,1024]{1,0:T(8,128)(2,1)S(1)}, u32[]{:S(2)}, u32[]{:S(2)}) collective-permute-start(bf16[48,1024]{1,0:T(8,128)(2,1)} %copy-done.6), channel_id=1, source_target_pairs={{0,13},{1,12},{2,15},{3,14},{4,9},{5,8},{6,11},{7,10},{8,5},{9,4},... | collective-permute-start | bytes 294920 | tf_op jit(solution)/shard_map/ppermute | solution.py:333
  132.2 9.8 %collective-permute-start.20 = (bf16[48,1024]{1,0:T(8,128)(2,1)}, bf16[48,1024]{1,0:T(8,128)(2,1)S(1)}, u32[]{:S(2)}, u32[]{:S(2)}) collective-permute-start(bf16[48,1024]{1,0:T(8,128)(2,1)} %copy-done.5), channel_id=1, source_target_pairs={{0,14},{1,15},{2,12},{3,13},{4,10},{5,11},{6,8},{7,9},{8,6},{9,7},... | collective-permute-start | bytes 294920 | tf_op jit(solution)/shard_map/ppermute | solution.py:333
  134.2 9.3 %collective-permute-start.21 = (bf16[48,1024]{1,0:T(8,128)(2,1)S(1)}, bf16[48,1024]{1,0:T(8,128)(2,1)S(1)}, u32[]{:S(2)}, u32[]{:S(2)}) collective-permute-start(bf16[48,1024]{1,0:T(8,128)(2,1)S(1)} %get-tuple-element.46), channel_id=1, source_target_pairs={{0,15},{1,14},{2,13},{3,12},{4,11},{5,10},{6,9},{7,8},{8,7},{9,6},... | collective-permute-start | bytes 294920 | tf_op jit(solution)/shard_map/ppermute | solution.py:333
  (11 other events, 7.0 us)
